TPU v7x, 512 devices: a whole 4x4x16 slice. The times are simulated.
512 devices in a mesh: section: 16 (over x_lo, y, core), seq: 32 (over x_hi, z).
Axes of the slice: x: 4 (x_hi: 2, x_lo: 2; x = x_hi * 2 + x_lo), y: 4, z: 16, core: 2. Of those that a mesh axis runs over, the one named last changes fastest.
Arguments:
- queries: bfloat16 [16, 256, 4096], P('section', 'seq'), may hold values from -110 to 110
- key_value_pages: bfloat16 [16, 64, 4, 2048], P('section', 'seq'), may hold values from -5 to 5
- block_table: int32 [16, 64], replicated, may hold values from 0 to 63, as said below
- page_mask: int32 [16, 1024], replicated, may hold values from 0 to 1, as said below
- noise_level: int32 [16], replicated, may hold values from 0 to 15
- level_gate: float32 [16, 4096], replicated, may hold values from 0.5 to 1.5
Outputs:
- attended: bfloat16 [16, 256, 4096], P('section', 'seq')
Inputs may be any that keep to these rules, and one draw needn't show every extreme that they name: `block_table`: each row is a permutation of 0 to 63. `page_mask`: a query span sees all pages of its own span, none of later spans, and some pages of earlier spans.
All inputs are finite; a program needn't handle non-finite values.
Results may differ from a plain program's by a relative error of at most 0.0065.
Values may be sent and summed in bfloat16 or wider, within the bound.
A program may use at most 64 MiB of HBM per device.

v0:
```python
import jax
import jax.numpy as jnp
from jax import lax
from jax.sharding import Mesh
from jax.sharding import PartitionSpec as P

QUERY_HEADS = 32
KEY_VALUE_HEADS = 8
HEAD_WIDTH = 128
SEQ = ("seq_0", "seq_1")


eps = 1e-06


def split_up(value, dim, peers):
    before, after = (value.shape[:dim], value.shape[dim + 1 :])
    return jnp.moveaxis(value.reshape(*before, peers, -1, *after), dim, 0)


def in_order(pieces, dim):
    pieces = jnp.moveaxis(pieces, 0, dim)
    shape = pieces.shape
    return pieces.reshape(*shape[:dim], shape[dim] * shape[dim + 1], *shape[dim + 2 :])


def exchange_in_order(pieces, axes, sequence):
    inside = pieces.shape[1:]
    filled = pieces.reshape(*(lax.axis_size(a) for a in axes), *inside)
    for k in sequence:
        filled = lax.all_to_all(filled, axes[k], k, k, tiled=True)
    return filled.reshape(-1, *inside)


def stepwise_exchange(value, axes, sequence, split_dim, concat_dim):
    pieces = split_up(value, split_dim, lax.axis_size(axes))
    return in_order(exchange_in_order(pieces, axes, sequence), concat_dim)


def body(queries, key_value_pages, block_table, page_mask, noise_level, level_gate):
    seq_count = lax.axis_size(SEQ)
    section_index = lax.axis_index("section")
    seq_index = lax.axis_index(SEQ)
    spans = page_mask.shape[0]
    pages = block_table.shape[1]
    page_length = key_value_pages.shape[2]
    span_group = QUERY_HEADS // KEY_VALUE_HEADS
    per_device = QUERY_HEADS // seq_count
    length = queries.shape[1] * seq_count
    scale = HEAD_WIDTH ** (-0.5)
    headed_queries = stepwise_exchange(queries, SEQ, (0, 1), 2, 1)
    query_rows = headed_queries.reshape(length, per_device, HEAD_WIDTH)
    onehot = (block_table[:, :, None] == jnp.arange(pages, dtype=jnp.int32)[None, None, :]).astype(
        jnp.float32
    )
    mask_row = lax.dynamic_index_in_dim(page_mask, section_index, 0, keepdims=False).reshape(
        spans, pages
    )
    visible = jnp.einsum("ci,cip->cp", mask_row.astype(jnp.float32), onehot)
    token_visible = jnp.repeat(visible, page_length, axis=1) > 0.5
    level_row = (
        jnp.arange(level_gate.shape[0], dtype=jnp.int32) == noise_level[section_index]
    ).astype(jnp.float32)
    gate_full = jnp.dot(level_row[None, :], level_gate, precision=lax.Precision.HIGHEST)[0].reshape(
        QUERY_HEADS, HEAD_WIDTH
    )
    gate_own = lax.dynamic_slice_in_dim(gate_full, seq_index * per_device, per_device, 0)

    def attend(carry, block, span):
        running, total, accum = carry
        keys = block[:, :, 0, :].reshape(length, per_device, HEAD_WIDTH)
        value_rows = block[:, :, 1, :].reshape(length, per_device, HEAD_WIDTH)
        seen = lax.dynamic_index_in_dim(token_visible, span, 0, keepdims=False)
        scores = (
            jnp.einsum("qhd,khd->qhk", query_rows, keys, preferred_element_type=jnp.float32) * scale
        )
        scores = jnp.where(seen[None, None, :], scores, -1e30)
        newmax = jnp.maximum(running, jnp.max(scores, axis=-1))
        shrink = jnp.exp(running - newmax)
        weights = jnp.where(seen[None, None, :], jnp.exp(scores - newmax[:, :, None]), 0.0)
        total = total * shrink + jnp.sum(weights, axis=-1)
        update = jnp.einsum(
            "qhk,khd->qhd",
            weights.astype(jnp.bfloat16),
            value_rows,
            preferred_element_type=jnp.float32,
        )
        accum = accum * shrink[:, :, None] + update
        return (newmax, total, accum)

    def visit(carry, block, span):
        return lax.cond(
            span <= section_index,
            lambda state: attend(state, block, span),
            lambda state: state,
            carry,
        )

    initial = (
        jnp.full((length, per_device), -1e30, jnp.float32),
        jnp.zeros((length, per_device), jnp.float32),
        jnp.zeros((length, per_device, HEAD_WIDTH), jnp.float32),
    )
    span_count = key_value_pages.shape[0]
    local_span_count = key_value_pages.shape[1]
    group_spread = key_value_pages.reshape(
        span_count, local_span_count, page_length, 2, KEY_VALUE_HEADS, 1, HEAD_WIDTH
    )
    group_spread = jnp.broadcast_to(
        group_spread,
        (span_count, local_span_count, page_length, 2, KEY_VALUE_HEADS, span_group, HEAD_WIDTH),
    )
    mine = stepwise_exchange(
        group_spread.reshape(
            span_count, local_span_count, page_length, 2, QUERY_HEADS * HEAD_WIDTH
        ),
        SEQ,
        (0, 1),
        4,
        1,
    )
    piece = lax.all_gather(mine, "section", axis=0, tiled=True)

    def inner(offset, state):
        block = lax.dynamic_index_in_dim(piece, offset, 0, keepdims=False)
        return visit(state, block, offset)

    carry = lax.fori_loop(0, piece.shape[0], inner, initial)
    running, total, accum = carry
    mixed = accum / total[:, :, None]
    normed = mixed * lax.rsqrt(jnp.mean(mixed * mixed, axis=-1, keepdims=True) + eps)
    gated = (
        (normed * gate_own[None, :, :])
        .astype(jnp.bfloat16)
        .reshape(1, length, per_device * HEAD_WIDTH)
    )
    return lax.all_to_all(gated, SEQ, split_axis=1, concat_axis=2, tiled=True)


def solution(mesh):
    finer = Mesh(mesh.devices.reshape(mesh.shape["section"], 2, 16), ("section", "seq_0", "seq_1"))
    in_specs = (P("section", SEQ, None), P("section", SEQ, None, None), P(), P(), P(), P())
    out_specs = P("section", SEQ, None)
    return jax.shard_map(body, mesh=finer, in_specs=in_specs, out_specs=out_specs, check_vma=False)
```

profile of v0, /device:TPU:27, one launch (start us, length us, event | category | flops | bytes accessed | tf_op | source)
XLA Modules:
  0.0 136.1 jit_solution(15695672740993060438)
XLA Ops:
  6.5 0.8 broadcast_in_dim.63
  7.5 7.7 %all_to_all.38 = bf16[2,16,1,2,4,2,128]{6,4,3,1,5,2,0:T(4,128)(2,1)S(1)} all-to-all(bf16[2,16,1,2,4,2,128]{6,4,3,1,5,2,0:T(4,128)(2,1)S(1)} %copy.19), channel_id=1, replica_groups=mesh['section'=16,'seq_0'=2,'seq_1'=16] {'seq_0'}, dimensions={0} | all-to-all | bytes 262144 | tf_op jit(solution)/shard_map/all_to_all | solution.py:31
  15.3 26.7 %all_to_all.39 = bf16[2,16,1,2,4,2,128]{6,4,3,0,5,2,1:T(4,128)(2,1)S(1)} all-to-all(bf16[2,16,1,2,4,2,128]{6,4,3,0,5,2,1:T(4,128)(2,1)S(1)} %copy.20), channel_id=1, replica_groups=mesh['section'=16,'seq_0'=2,'seq_1'=16] {'seq_1'}, dimensions={1} | all-to-all | bytes 262144 | tf_op jit(solution)/shard_map/all_to_all | solution.py:31
  42.0 0.8 copy.21
  42.8 3.3 %all-to-all-start.2 = ((bf16[2,16,1,8,128]{4,3,1,2,0:T(8,128)(2,1)}), bf16[2,16,1,8,128]{4,3,1,2,0:T(8,128)(2,1)S(1)}, u32[]{:S(2)}, u32[]{:S(2)}) async-start(bf16[2,16,1,8,128]{4,3,1,2,0:T(8,128)(2,1)} %bitcast.92), calls=%async_computation.2 | async-start | bytes 131072 | tf_op jit(solution)/shard_map/all_to_all | solution.py:31
  46.1 0.8 convert_reduce_fusion
  47.0 1.2 dynamic_slice.30
  48.2 0.9 fusion.15
  49.1 0.3 fusion.14
  49.4 1.2 all-to-all-done.2
  50.6 0.6 copy.22
  51.2 4.0 %all-to-all-start.3 = ((bf16[2,16,1,8,128]{4,3,0,2,1:T(8,128)(2,1)}), bf16[2,16,1,8,128]{4,3,0,2,1:T(8,128)(2,1)S(1)}, u32[]{:S(2)}, u32[]{:S(2)}) async-start(bf16[2,16,1,8,128]{4,3,0,2,1:T(8,128)(2,1)} %copy.22), calls=%async_computation.3 | async-start | bytes 131072 | tf_op jit(solution)/shard_map/all_to_all | solution.py:31
  55.4 11.5 %all-to-all-done.3 = bf16[2,16,1,8,128]{4,3,0,2,1:T(8,128)(2,1)S(1)} async-done(((bf16[2,16,1,8,128]{4,3,0,2,1:T(8,128)(2,1)}), bf16[2,16,1,8,128]{4,3,0,2,1:T(8,128)(2,1)S(1)}, u32[]{:S(2)}, u32[]{:S(2)}) %all-to-all-start.3) | async-done | bytes 65568 | tf_op jit(solution)/shard_map/all_to_all | solution.py:31
  66.8 10.6 %all-gather.2.cloned.1.call-done = bf16[16,64,4,2,128]{4,1,3,2,0:T(8,128)(2,1)} async-done(((bf16[1,64,4,2,128]{4,1,3,2,0:T(8,128)(2,1)}), bf16[16,64,4,2,128]{4,1,3,2,0:T(8,128)(2,1)}) %all-gather.2.cloned.1.call-update) | async-done | bytes 2097168 | tf_op jit(solution)/shard_map/all_gather | solution.py:122
  77.4 3.6 %copy.24 = bf16[16,64,4,2,128]{4,2,1,3,0:T(4,128)(2,1)S(1)} copy(bf16[16,64,4,2,128]{4,1,3,2,0:T(8,128)(2,1)} %all-gather.2.cloned.1.call-done) | data formatting | bytes 4194304
  81.0 15.7 %while.18 = (s32[]{:T(128)}, f32[256,1]{0,1:T(1,128)S(1)}, f32[256,1]{0,1:T(1,128)S(1)}, f32[256,1,128]{0,2,1:T(8,128)S(1)}, s32[]{:T(128)}, /*index=5*/bf16[16,...) while((s32[]{:T(128)}, f32[256,1]{0,1:T(1,128)S(1)}, ...), condition=%wide.region_5.6_spmd.clone, body=%wide.region_0.5_spmd.clone.sunk | while | flops 34210312 | bytes 1800709 | solution.py:128
  81.1 0.9 conditional.3
  82.1 0.9 conditional.3
  82.7 0.3 fusion.4
  83.1 0.9 conditional.3
  83.7 0.3 fusion.4
  84.0 0.9 conditional.3
  85.0 0.9 conditional.3
  85.6 0.3 fusion.4
  86.0 0.9 conditional.3
  86.6 0.3 fusion.4
  87.0 0.9 conditional.3
  87.6 0.3 fusion.4
  88.0 0.9 conditional.3
  88.6 0.3 fusion.4
  88.9 0.9 conditional.3
  89.6 0.3 fusion.4
  89.9 0.9 conditional.3
  90.5 0.3 fusion.4
  90.9 0.9 conditional.3
  91.5 0.3 fusion.4
  91.9 0.9 conditional.3
  92.9 0.9 conditional.3
  93.5 0.3 fusion.4
  93.8 0.9 conditional.3
  94.5 0.3 fusion.4
  94.8 0.9 conditional.3
  95.4 0.3 fusion.4
  95.8 0.9 conditional.3
  97.3 0.5 broadcast.53
  97.8 1.0 reduce.15
  98.9 29.7 %all_to_all.40 = bf16[32,2,512]{2,1,0:T(2,128)(2,1)S(1)} all-to-all(bf16[32,2,512]{2,1,0:T(2,128)(2,1)S(1)} %reshape.119), channel_id=1, replica_groups=mesh['section'=16,'seq_0'=2,'seq_1'=16] {'seq_0','seq_1'}, dimensions={0} | all-to-all | bytes 131072 | tf_op jit(solution)/shard_map/all_to_all | solution.py:137
  128.6 0.6 copy.39
  (188 shorter events, 11.9 us)
Async XLA Ops:
  6.5 41.7 %copy-start = (f32[16,4096]{1,0:T(8,128)S(1)}, f32[16,4096]{1,0:T(8,128)}, u32[]{:S(2)}) copy-start(f32[16,4096]{1,0:T(8,128)} %param.15) | copy-start | bytes 786436
  6.5 42.5 %copy-start.1 = (s32[16,64]{1,0:T(8,128)S(1)}, s32[16,64]{1,0:T(8,128)}, u32[]{:S(2)}) copy-start(s32[16,64]{1,0:T(8,128)} %param.12) | copy-start | bytes 12292
  6.5 70.9 %all-gather.2.cloned.1.call-start = ((), (), s32[]{:S(2)}) async-start(), calls=%async_computation.5 | async-start | bytes 2228224 | tf_op jit(solution)/shard_map/all_gather | solution.py:122
  42.8 7.8 %all-to-all-start.2 = ((bf16[2,16,1,8,128]{4,3,1,2,0:T(8,128)(2,1)}), bf16[2,16,1,8,128]{4,3,1,2,0:T(8,128)(2,1)S(1)}, u32[]{:S(2)}, u32[]{:S(2)}) async-start(bf16[2,16,1,8,128]{4,3,1,2,0:T(8,128)(2,1)} %bitcast.92), calls=%async_computation.2 | async-start | bytes 131072 | tf_op jit(solution)/shard_map/all_to_all | solution.py:31
  51.2 15.6 %all-to-all-start.3 = ((bf16[2,16,1,8,128]{4,3,0,2,1:T(8,128)(2,1)}), bf16[2,16,1,8,128]{4,3,0,2,1:T(8,128)(2,1)S(1)}, u32[]{:S(2)}, u32[]{:S(2)}) async-start(bf16[2,16,1,8,128]{4,3,0,2,1:T(8,128)(2,1)} %copy.22), calls=%async_computation.3 | async-start | bytes 131072 | tf_op jit(solution)/shard_map/all_to_all | solution.py:31
Sparse Core Ops, SparseCore 0:
  42.9 34.4 all-gather.1
where the time goes:
time: 137 us; the launch traced here: 136 us
  blocking collectives  64.1 us (47%)
  waiting for transfers between devices  23.3 us (17%)
  between operations  13.5 us (10%)
  local copies, waits for them, and re-layouts  12.8 us (9%)
  matrix products  9.12 us (7%)
  starting transfers between devices  7.34 us (5%)
  other arithmetic  4.47 us (3%)
  loops' own time  1.48 us (1%)
    all_to_all x2, blocking collectives, exchange_in_order(): filled = lax.all_to_all(filled, axes[k], k, k, tiled=True)  34.4 us
    all_to_all x1, blocking collectives, body(): return lax.all_to_all(gated, SEQ, split_axis=1, concat_axis=2, tiled=True)  29.7 us
    all_to_all x2, waiting for transfers between devices, exchange_in_order(): filled = lax.all_to_all(filled, axes[k], k, k, tiled=True)  12.6 us
    all_gather x1, waiting for transfers between devices, body(): piece = lax.all_gather(mine, 'section', axis=0, tiled=True)  10.6 us
    all_to_all x2, starting transfers between devices, exchange_in_order(): filled = lax.all_to_all(filled, axes[k], k, k, tiled=True)  7.34 us
    unnamed x9, local copies, waits for them, and re-layouts  4.81 us
    dot_general x16, matrix products, attend(): jnp.einsum('qhk,khd->qhd', weights.astype(jnp.bfloat16), value_rows, pref...  4.43 us
    dot_general x16, matrix products, attend(): jnp.einsum('qhd,khd->qhk', query_rows, keys, preferred_element_type=jnp.f...  3.53 us
  transfers between devices with their start and end apart: 3, of which 3 were waited for; matrix products, arithmetic and copies ran while one was open for 3% of the time, Pallas kernels for 0%

commit v1 on v0

v1 whole, which is shorter than its diff:
```python
import functools

import jax
import jax.numpy as jnp
from jax import lax
from jax.experimental import pallas as pl
from jax.experimental.pallas import tpu as pltpu
from jax.sharding import PartitionSpec as P

QUERY_HEADS = 32
KEY_VALUE_HEADS = 8
HEAD_WIDTH = 128
SPANS = 16
PAGES = 64
PARTS = 4
PEERS = 8
RUN = 8
GROUP = QUERY_HEADS // KEY_VALUE_HEADS
WIDE = GROUP * HEAD_WIDTH
ROWS = GROUP * PEERS * RUN
SPAN = PARTS * PEERS * RUN
EXPONENT = HEAD_WIDTH ** (-0.5) * 1.4426950408889634
HIDDEN = -3e30
MESH = pl.DeviceIdType.MESH

eps = 1e-06


def kernel(
    queries,
    source,
    table,
    mask,
    noise,
    gates,
    out,
    kv,
    arrived,
    rows,
    ready,
    gate,
    bias,
    top,
    total,
    accum,
    spread_send,
    spread_recv,
    query_send,
    query_recv,
    gate_sem,
    relay_send,
    relay_recv,
    pair_recv,
    out_send,
    out_recv,
):
    s = lax.axis_index("section")
    t = lax.axis_index("seq")
    chip, core = s // 2, s % 2
    x, y = chip // 4, chip % 4
    part = (t % 16) // 4
    me = (t // 16) * 4 + t % 4

    def seat(peer, block):
        return (peer // 4) * 16 + block * 4 + peer % 4

    def section(xx, yy):
        return (xx * 4 + yy) * 2 + core

    up, down = (y + 1) % 4, (y + 3) % 4
    partner = chip * 2 + 1 - core

    barrier = pltpu.get_barrier_semaphore()
    for step in range(1, 32):
        pl.semaphore_signal(barrier, inc=1, device_id=(s, (t + step) % 32), device_id_type=MESH)
    for other in (section(x, up), section(x, down), section(1 - x, y), partner):
        pl.semaphore_signal(barrier, inc=1, device_id=(other, t), device_id_type=MESH)

    gate_copy = pltpu.make_async_copy(
        gates.at[:, pl.ds(pl.multiple_of(me * WIDE, WIDE), WIDE)], gate, gate_sem
    )
    gate_copy.start()

    place = lax.broadcasted_iota(jnp.int32, (SPAN, PAGES), 0)
    holder = ((place // 32) % 2) * 16 + (place // 64) * 4 + (place // 8) % 4
    page = holder * 2 + (place % 8) // 4
    wanted = mask[pl.ds(s, 1), :].astype(jnp.float32)
    for c in range(SPANS):
        onehot = (table[c : c + 1, :] == page).astype(jnp.float32)
        row = jnp.broadcast_to(wanted[:, c * PAGES : (c + 1) * PAGES], (8, PAGES))
        seen = lax.dot_general(row, onehot, (((1,), (1,)), ((), ())))
        bias[c] = jnp.where(seen > 0.5, 0.0, HIDDEN)

    pl.semaphore_wait(barrier, 35)

    sends = []
    local = None
    for turn in (0, 1, 3, 2):
        block = (part + turn) % PARTS
        for step in range(PEERS):
            peer = (me + step) % PEERS
            if turn == 0 and step == 0:
                local = pltpu.make_async_copy(
                    source.at[peer], kv.at[s, part, :, me], spread_recv.at[part]
                )
                local.start()
                continue
            copy = pltpu.make_async_remote_copy(
                src_ref=source.at[peer],
                dst_ref=kv.at[s, part, :, me],
                send_sem=spread_send.at[turn * PEERS + step],
                recv_sem=spread_recv.at[part],
                device_id=(s, seat(peer, block)),
                device_id_type=MESH,
            )
            copy.start()
            sends.append((None, copy))
    for step in range(PEERS):
        peer = (me + step) % PEERS
        piece = queries.at[0, :, pl.ds(pl.multiple_of(peer * WIDE, WIDE), WIDE)]
        if step == 0:
            pltpu.make_async_copy(piece, arrived.at[me], query_recv).start()
            continue
        copy = pltpu.make_async_remote_copy(
            src_ref=piece,
            dst_ref=arrived.at[me],
            send_sem=query_send.at[step],
            recv_sem=query_recv,
            device_id=(s, seat(peer, part)),
            device_id_type=MESH,
        )
        copy.start()
        sends.append((None, copy))

    count = [0]

    def relay(slot, piece, other, condition):
        number = count[0]
        count[0] += 1
        copy = pltpu.make_async_remote_copy(
            src_ref=kv.at[slot, piece],
            dst_ref=kv.at[slot, piece],
            send_sem=relay_send.at[number],
            recv_sem=relay_recv.at[slot, piece],
            device_id=(other, t),
            device_id_type=MESH,
        )

        @pl.when(condition)
        def _():
            copy.start()

        sends.append((condition, copy))

    def share(slot, condition):
        number = count[0]
        count[0] += 1
        copy = pltpu.make_async_remote_copy(
            src_ref=kv.at[slot],
            dst_ref=kv.at[slot],
            send_sem=relay_send.at[number],
            recv_sem=pair_recv.at[slot],
            device_id=(partner, t),
            device_id_type=MESH,
        )

        @pl.when(condition)
        def _():
            copy.start()

        sends.append((condition, copy))

    def landed(slot, piece, condition):
        @pl.when(condition)
        def _():
            pltpu.make_async_copy(
                kv.at[slot, piece], kv.at[slot, piece], relay_recv.at[slot, piece]
            ).wait()

    def shared(slot, condition):
        @pl.when(condition)
        def _():
            pltpu.make_async_copy(kv.at[slot], kv.at[slot], pair_recv.at[slot]).wait()

    def attend(first, spans, condition):
        @pl.when(condition)
        def _():
            keys = jnp.concatenate(
                [kv[first + n, :, 0].reshape(SPAN, HEAD_WIDTH) for n in range(spans)], axis=0
            )
            values = jnp.concatenate(
                [kv[first + n, :, 1].reshape(SPAN, HEAD_WIDTH) for n in range(spans)], axis=0
            )
            hide = jnp.concatenate([bias[first + n, 0:1, :] for n in range(spans)], axis=1)
            scores = lax.dot_general(
                rows[...], keys, (((1,), (1,)), ((), ())), preferred_element_type=jnp.float32
            )
            scores = scores + hide
            before = top[...]
            after = jnp.maximum(before, jnp.max(scores, axis=1, keepdims=True))
            shrink = jnp.exp2((before - after) * EXPONENT)
            weights = jnp.exp2((scores - after) * EXPONENT)
            top[...] = after
            total[...] = total[...] * shrink + jnp.sum(weights, axis=1, keepdims=True)
            accum[...] = accum[...] * shrink + jnp.dot(
                weights.astype(jnp.bfloat16), values, preferred_element_type=jnp.float32
            )

    always = s >= 0
    order = [(part + turn) % PARTS for turn in (0, 1, 3, 2)]

    for piece in order:
        pltpu.make_async_copy(kv.at[s, piece], kv.at[s, piece], spread_recv.at[piece]).wait()
        relay(s, piece, section(x, up), (x == 0) | (y < 3))
        relay(s, piece, section(1, y), x == 0)
        relay(s, piece, section(x, down), y == 0)
    share(s, core == 0)

    pltpu.make_async_copy(arrived, arrived, query_recv).wait()
    for head in range(GROUP):
        lanes = slice(head * HEAD_WIDTH, (head + 1) * HEAD_WIDTH)
        tall = arrived[:, :, lanes].astype(jnp.float32).reshape(PEERS * RUN, HEAD_WIDTH)
        rows[head * PEERS * RUN : (head + 1) * PEERS * RUN, :] = tall.astype(jnp.bfloat16)
    top[...] = jnp.full(top.shape, -1e30, jnp.float32)
    total[...] = jnp.zeros(total.shape, jnp.float32)
    accum[...] = jnp.zeros(accum.shape, jnp.float32)
    attend(s, 1, always)

    chip0 = x * 4 + down
    slot0, gets0, uses0 = chip0 * 2 + core, (x == 0) | (y >= 1), y >= 1
    chip3 = y
    slot3 = chip3 * 2 + core
    far = x == 1
    for piece in order:
        landed(slot0, piece, gets0)
        relay(slot0, piece, section(1, y), x == 0)
        relay(slot0, piece, section(x, up), (y == 1) | (y == 2))
        landed(slot3, piece, far)
        relay(slot3, piece, section(1, down), far)
    share(slot0, uses0)
    share(slot3, far)

    chip4 = down
    slot4 = chip4 * 2 + core
    for piece in order:
        landed(slot4, piece, far)
        relay(slot4, piece, section(1, up), far)
    share(slot4, far)

    shared(chip * 2, core == 1)
    attend(chip * 2, 1, core == 1)

    def take(which, condition):
        shared(which * 2 + 1 - core, condition)
        attend(which * 2, 2, condition)

    def tail(which, condition):
        slot = which * 2 + core
        for piece in order:
            landed(slot, piece, condition)
        share(slot, condition)

    chip1, uses1 = x * 4, y == 3
    chip2, uses2 = x * 4 + (y + 2) % 4, y >= 2
    chip5, chip6 = up, (y + 2) % 4
    take(chip0, uses0)
    tail(chip1, uses1)
    tail(chip2, uses2)
    take(chip3, far)
    tail(chip5, far)
    take(chip1, uses1)
    take(chip2, uses2)
    take(chip4, far)
    tail(chip6, far)
    take(chip5, far)
    take(chip6, far)

    gate_copy.wait()
    level = noise[s]
    row = gate[pl.ds(level, 1), :]
    mixed = accum[...] / total[...]
    normed = mixed * lax.rsqrt(jnp.mean(mixed * mixed, axis=1, keepdims=True) + eps)
    for head in range(GROUP):
        lanes = slice(head * HEAD_WIDTH, (head + 1) * HEAD_WIDTH)
        block = normed[head * PEERS * RUN : (head + 1) * PEERS * RUN, :] * row[:, lanes]
        ready[:, :, lanes] = block.reshape(PEERS, RUN, HEAD_WIDTH).astype(jnp.bfloat16)
    mine = out.at[0, :, pl.ds(pl.multiple_of(me * WIDE, WIDE), WIDE)]
    for step in range(PEERS):
        peer = (me + step) % PEERS
        if step == 0:
            pltpu.make_async_copy(ready.at[peer], mine, out_recv).start()
            continue
        copy = pltpu.make_async_remote_copy(
            src_ref=ready.at[peer],
            dst_ref=mine,
            send_sem=out_send.at[step],
            recv_sem=out_recv,
            device_id=(s, seat(peer, part)),
            device_id_type=MESH,
        )
        copy.start()
        sends.append((None, copy))

    for condition, copy in sends:
        if condition is None:
            copy.wait_send()
        else:
            pl.when(condition)(copy.wait_send)
    pltpu.make_async_copy(out, out, out_recv).wait()


def body(queries, key_value_pages, block_table, page_mask, noise_level, level_gate):
    source = key_value_pages.reshape(RUN, 2, KEY_VALUE_HEADS, HEAD_WIDTH).transpose(2, 1, 0, 3)
    vmem = pl.BlockSpec(memory_space=pltpu.VMEM)
    anywhere = pl.BlockSpec(memory_space=pl.ANY)
    dma = pltpu.SemaphoreType.DMA
    return pl.pallas_call(
        kernel,
        out_shape=jax.ShapeDtypeStruct(queries.shape, jnp.bfloat16),
        in_specs=[
            anywhere,
            anywhere,
            vmem,
            vmem,
            pl.BlockSpec(memory_space=pltpu.SMEM),
            anywhere,
        ],
        out_specs=vmem,
        scratch_shapes=[
            pltpu.VMEM((SPANS, PARTS, 2, PEERS, RUN, HEAD_WIDTH), jnp.bfloat16),
            pltpu.VMEM((PEERS, RUN, WIDE), jnp.bfloat16),
            pltpu.VMEM((ROWS, HEAD_WIDTH), jnp.bfloat16),
            pltpu.VMEM((PEERS, RUN, WIDE), jnp.bfloat16),
            pltpu.VMEM((level_gate.shape[0], WIDE), jnp.float32),
            pltpu.VMEM((SPANS, 8, SPAN), jnp.float32),
            pltpu.VMEM((ROWS, 1), jnp.float32),
            pltpu.VMEM((ROWS, 1), jnp.float32),
            pltpu.VMEM((ROWS, HEAD_WIDTH), jnp.float32),
            dma((32,)),
            dma((PARTS,)),
            dma((PEERS,)),
            dma,
            dma,
            dma((64,)),
            dma((SPANS, PARTS)),
            dma((SPANS,)),
            dma((PEERS,)),
            dma,
        ],
        compiler_params=pltpu.CompilerParams(collective_id=0, has_side_effects=True),
    )(queries, source, block_table, page_mask, noise_level, level_gate)


def solution(mesh):
    in_specs = (P("section", "seq", None), P("section", "seq", None, None), P(), P(), P(), P())
    out_specs = P("section", "seq", None)
    return jax.shard_map(body, mesh=mesh, in_specs=in_specs, out_specs=out_specs, check_vma=False)
```

time: 137 us -> 50.2 us (0.37)
  the two profiles are of different devices: /device:TPU:27 before, /device:TPU:3 now
where the time goes in v1:
time: 50.2 us; the launch traced here: 49.9 us
  Pallas kernels  47 us (94%)
  local copies, waits for them, and re-layouts  2.88 us (6%)
    pallas_call x1, Pallas kernels, body(): pl.pallas_call(kernel, out_shape=jax.ShapeDtypeStruct(queries.shape, jnp....  47 us
    unnamed x1, local copies, waits for them, and re-layouts  1.47 us
    reshape x2, local copies, waits for them, and re-layouts, body(): key_value_pages.reshape(RUN, 2, KEY_VALUE_HEADS, HEAD_WIDTH)  1.41 us

profile of v1, /device:TPU:3, one launch (start us, length us, event | category | flops | bytes accessed | tf_op | source)
XLA Modules:
  0.0 49.9 jit_solution(10007082189903315986)
XLA Ops:
  0.0 0.8 %reshape.3 = bf16[8,2,8,128]{3,2,1,0:T(8,128)(2,1)S(1)} reshape(bf16[1,2,4,2048]{3,2,1,0:T(4,128)(2,1)} %param.7) | data formatting | bytes 65536 | tf_op jit(solution)/shard_map/reshape | solution.py:313
  0.8 0.6 %copy.9 = bf16[8,2,8,128]{3,0,1,2:T(8,128)(2,1)} copy(bf16[8,2,8,128]{3,2,1,0:T(8,128)(2,1)S(1)} %reshape.3) | data formatting | bytes 65536 | tf_op jit(solution)/shard_map/reshape | solution.py:313
  1.4 47.0 %shard_map.64 = bf16[1,8,4096]{2,1,0:T(8,128)(2,1)} custom-call(bf16[1,8,4096]{2,1,0:T(8,128)(2,1)} %queries.1, bf16[8,2,8,128]{3,2,1,0:T(8,128)(2,1)} %bitcast.3, s32[16,64]{1,0:T(8,128)} %table.1, s32[16,1024]{1,0:T(8,128)} %mask.1, s32[16]{0:T(128)} %noise.1, f32[16,4096]{1,0:T(8,128)} %gates.1), custom_call_target="tpu_custom_call" | custom-call | tf_op jit(solution)/shard_map/pallas_call | solution.py:317
  48.4 1.5 %copy.11 = bf16[1,8,4096]{2,1,0:T(8,128)(2,1)} copy(bf16[1,8,4096]{2,1,0:T(8,128)(2,1)} %shard_map.64) | data formatting | bytes 131072

commit v2 on v1

v2 whole, which is shorter than its diff:
```python
import functools

import jax
import jax.numpy as jnp
from jax import lax
from jax.experimental import pallas as pl
from jax.experimental.pallas import tpu as pltpu
from jax.sharding import PartitionSpec as P

QUERY_HEADS = 32
KEY_VALUE_HEADS = 8
HEAD_WIDTH = 128
SPANS = 16
PAGES = 64
PARTS = 4
PEERS = 8
RUN = 8
GROUP = QUERY_HEADS // KEY_VALUE_HEADS
WIDE = GROUP * HEAD_WIDTH
ROWS = GROUP * PEERS * RUN
SPAN = PARTS * PEERS * RUN
EXPONENT = HEAD_WIDTH ** (-0.5) * 1.4426950408889634
HIDDEN = -3e30
MESH = pl.DeviceIdType.MESH

eps = 1e-06


def kernel(
    queries,
    pool,
    table_any,
    mask_any,
    noise,
    gates,
    out,
    kv,
    arrived,
    rows,
    ready,
    gate,
    raw,
    source,
    table,
    mask,
    bias,
    top,
    total,
    accum,
    local_sem,
    spread_send,
    spread_recv,
    query_send,
    query_recv,
    deep_send,
    deep_recv,
    half_recv,
    relay_send,
    relay_recv,
    share_send,
    share_recv,
    out_send,
    out_recv,
):
    s = lax.axis_index("section")
    t = lax.axis_index("seq")
    chip, core = s // 2, s % 2
    x, y = chip // 4, chip % 4
    column, z = t // 16, t % 16
    part = z // 4
    me = column * 4 + z % 4

    def seat(peer):
        return (peer // 4) * 16 + part * 4 + peer % 4

    def section(xx, yy):
        return (xx * 4 + yy) * 2 + core

    up, down = (y + 1) % 4, (y + 3) % 4
    partner = chip * 2 + 1 - core
    ahead, behind = column * 16 + (z + 4) % 16, column * 16 + (z + 12) % 16

    barrier = pltpu.get_barrier_semaphore()
    near = [(s, seat((me + step) % PEERS)) for step in range(1, PEERS)]
    near += [(s, ahead), (s, behind)]
    near += [(other, t) for other in (section(x, up), section(x, down), section(1 - x, y), partner)]
    for other in near:
        pl.semaphore_signal(barrier, inc=1, device_id=other, device_id_type=MESH)

    mine = pl.ds(pl.multiple_of(me * WIDE, WIDE), WIDE)
    loads = [
        pltpu.make_async_copy(pool.at[0], raw, local_sem.at[0]),
        pltpu.make_async_copy(table_any, table, local_sem.at[1]),
        pltpu.make_async_copy(mask_any, mask, local_sem.at[2]),
        pltpu.make_async_copy(gates.at[:, mine], gate, local_sem.at[3]),
    ]
    for load in loads:
        load.start()

    loads[0].wait()
    for head in range(KEY_VALUE_HEADS):
        for kind in range(2):
            first = (kind * KEY_VALUE_HEADS + head) * HEAD_WIDTH
            for page in range(2):
                source[head, kind, page * 4 : (page + 1) * 4, :] = raw[
                    page, :, first : first + HEAD_WIDTH
                ]

    @pl.when(core == 0)
    def _():
        kv[s + 1] = jnp.zeros(kv.shape[1:], kv.dtype)

    top[...] = jnp.full(top.shape, -1e30, jnp.float32)
    total[...] = jnp.zeros(total.shape, jnp.float32)
    accum[...] = jnp.zeros(accum.shape, jnp.float32)

    pl.semaphore_wait(barrier, len(near))

    sends = []
    pltpu.make_async_copy(source.at[me], kv.at[s, part, :, me], spread_recv).start()
    for step in range(1, PEERS):
        peer = (me + step) % PEERS
        copy = pltpu.make_async_remote_copy(
            src_ref=source.at[peer],
            dst_ref=kv.at[s, part, :, me],
            send_sem=spread_send.at[step],
            recv_sem=spread_recv,
            device_id=(s, seat(peer)),
            device_id_type=MESH,
        )
        copy.start()
        sends.append((None, copy))
    for step in range(PEERS):
        peer = (me + step) % PEERS
        piece = queries.at[0, :, pl.ds(pl.multiple_of(peer * WIDE, WIDE), WIDE)]
        if step == 0:
            pltpu.make_async_copy(piece, arrived.at[me], query_recv).start()
            continue
        copy = pltpu.make_async_remote_copy(
            src_ref=piece,
            dst_ref=arrived.at[me],
            send_sem=query_send.at[step],
            recv_sem=query_recv,
            device_id=(s, seat(peer)),
            device_id_type=MESH,
        )
        copy.start()
        sends.append((None, copy))

    loads[1].wait()
    loads[2].wait()
    place = lax.broadcasted_iota(jnp.int32, (SPAN, PAGES), 0)
    holder = ((place // 32) % 2) * 16 + (place // 64) * 4 + (place // 8) % 4
    page = holder * 2 + (place % 8) // 4
    wanted = mask[pl.ds(s, 1), :].astype(jnp.float32)
    for c in range(SPANS):
        onehot = (table[c : c + 1, :] == page).astype(jnp.float32)
        row = jnp.broadcast_to(wanted[:, c * PAGES : (c + 1) * PAGES], (8, PAGES))
        seen = lax.dot_general(row, onehot, (((1,), (1,)), ((), ())))
        hide = jnp.where(seen > 0.5, 0.0, HIDDEN)
        lanes = slice((c % 2) * 64, (c % 2) * 64 + 64)
        for piece in range(PARTS):
            bias[c // 2, piece, :, lanes] = hide[:, piece * 64 : (piece + 1) * 64]

    def deep(src, number, arrival, other):
        copy = pltpu.make_async_remote_copy(
            src_ref=src,
            dst_ref=src,
            send_sem=deep_send.at[number],
            recv_sem=arrival,
            device_id=(s, other),
            device_id_type=MESH,
        )
        copy.start()
        sends.append((None, copy))

    count = [0, 0]

    def relay(slot, piece, other, condition):
        copy = pltpu.make_async_remote_copy(
            src_ref=kv.at[slot, piece],
            dst_ref=kv.at[slot, piece],
            send_sem=relay_send.at[count[0]],
            recv_sem=relay_recv.at[slot, piece],
            device_id=(other, t),
            device_id_type=MESH,
        )
        count[0] += 1
        pl.when(condition)(copy.start)
        sends.append((condition, copy))

    def share(slot, piece, condition):
        copy = pltpu.make_async_remote_copy(
            src_ref=kv.at[slot, piece],
            dst_ref=kv.at[slot, piece],
            send_sem=share_send.at[count[1]],
            recv_sem=share_recv.at[slot, piece],
            device_id=(partner, t),
            device_id_type=MESH,
        )
        count[1] += 1
        pl.when(condition)(copy.start)
        sends.append((condition, copy))

    def arrival(ref, sem):
        pltpu.make_async_copy(ref, ref, sem).wait()

    def landed(slot, piece, condition):
        @pl.when(condition)
        def _():
            arrival(kv.at[slot, piece], relay_recv.at[slot, piece])

    def attend(which, pieces, condition):
        @pl.when(condition)
        def _():
            units = [(which * 2 + n, piece) for piece in pieces for n in range(2)]
            keys, values = (
                jnp.concatenate(
                    [kv[a, b, kind].reshape(PEERS * RUN, HEAD_WIDTH) for a, b in units], axis=0
                )
                for kind in range(2)
            )
            hide = jnp.concatenate([bias[which, piece, 0:1, :] for piece in pieces], axis=1)
            scores = lax.dot_general(
                rows[...], keys, (((1,), (1,)), ((), ())), preferred_element_type=jnp.float32
            )
            scores = scores + hide
            before = top[...]
            after = jnp.maximum(before, jnp.max(scores, axis=1, keepdims=True))
            shrink = jnp.exp2((before - after) * EXPONENT)
            weights = jnp.exp2((scores - after) * EXPONENT)
            top[...] = after
            total[...] = total[...] * shrink + jnp.sum(weights, axis=1, keepdims=True)
            accum[...] = accum[...] * shrink + jnp.dot(
                weights.astype(jnp.bfloat16), values, preferred_element_type=jnp.float32
            )

    always = s >= 0
    far = x == 1
    first, after1, before1, opposite = (part + 0, (part + 1) % 4, (part + 3) % 4, (part + 2) % 4)

    def outward(piece):
        relay(s, piece, section(x, up), (x == 0) | (y < 3))
        relay(s, piece, section(1, y), x == 0)
        relay(s, piece, section(x, down), y == 0)
        share(s, piece, core == 0)

    chip0, chip1, chip2 = x * 4 + down, x * 4, x * 4 + (y + 2) % 4
    chip3, chip4, chip5, chip6 = y, down, up, (y + 2) % 4
    gets0, uses0, uses1, uses2 = (x == 0) | (y >= 1), y >= 1, y == 3, y >= 2

    def early(piece):
        slot = chip0 * 2 + core
        landed(slot, piece, gets0)
        relay(slot, piece, section(1, y), x == 0)
        relay(slot, piece, section(x, up), (y == 1) | (y == 2))
        share(slot, piece, uses0)
        slot = chip3 * 2 + core
        landed(slot, piece, far)
        relay(slot, piece, section(1, down), far)
        share(slot, piece, far)

    def middle(piece):
        slot = chip4 * 2 + core
        landed(slot, piece, far)
        relay(slot, piece, section(1, up), far)
        share(slot, piece, far)

    def late(piece, which, condition):
        slot = which * 2 + core
        landed(slot, piece, condition)
        share(slot, piece, condition)

    def tail(piece):
        late(piece, chip1, uses1)
        late(piece, chip2, uses2)
        late(piece, chip5, far)
        late(piece, chip6, far)

    def take(which, pieces, condition):
        slot = which * 2 + 1 - core
        for piece in pieces:

            @pl.when(condition)
            def _():
                arrival(kv.at[slot, piece], share_recv.at[slot, piece])

        attend(which, pieces, condition)

    def own(pieces):
        for piece in pieces:

            @pl.when(core == 1)
            def _():
                arrival(kv.at[chip * 2, piece], share_recv.at[chip * 2, piece])

        attend(chip, pieces, always)

    arrival(kv.at[s, first], spread_recv)
    deep(kv.at[s, first], 0, deep_recv.at[0], ahead)
    deep(kv.at[s, first], 1, deep_recv.at[1], behind)
    outward(first)

    arrival(arrived, query_recv)
    for head in range(GROUP):
        lanes = slice(head * HEAD_WIDTH, (head + 1) * HEAD_WIDTH)
        tall = arrived[:, :, lanes].astype(jnp.float32).reshape(PEERS * RUN, HEAD_WIDTH)
        rows[head * PEERS * RUN : (head + 1) * PEERS * RUN, :] = tall.astype(jnp.bfloat16)

    early(first)
    arrival(kv.at[s, before1], deep_recv.at[0])
    deep(kv.at[s, before1, 0], 2, half_recv.at[0], ahead)
    outward(before1)
    arrival(kv.at[s, after1], deep_recv.at[1])
    deep(kv.at[s, after1, 1], 3, half_recv.at[1], behind)
    outward(after1)
    middle(first)
    early(before1)
    early(after1)
    arrival(kv.at[s, opposite, 0], half_recv.at[0])
    arrival(kv.at[s, opposite, 1], half_recv.at[1])
    outward(opposite)
    middle(before1)
    middle(after1)
    tail(first)
    early(opposite)
    most = (first, before1, after1)
    own(most)
    take(chip0, most, uses0)
    middle(opposite)
    tail(before1)
    tail(after1)
    take(chip3, most, far)
    take(chip4, most, far)
    take(chip1, most, uses1)
    take(chip2, most, uses2)
    take(chip5, most, far)
    take(chip6, most, far)
    last = (opposite,)
    tail(opposite)
    own(last)
    take(chip0, last, uses0)
    take(chip3, last, far)
    take(chip4, last, far)
    take(chip1, last, uses1)
    take(chip2, last, uses2)
    take(chip5, last, far)
    take(chip6, last, far)

    loads[3].wait()
    level = noise[s]
    row = gate[pl.ds(level, 1), :]
    mixed = accum[...] / total[...]
    normed = mixed * lax.rsqrt(jnp.mean(mixed * mixed, axis=1, keepdims=True) + eps)
    for head in range(GROUP):
        lanes = slice(head * HEAD_WIDTH, (head + 1) * HEAD_WIDTH)
        block = normed[head * PEERS * RUN : (head + 1) * PEERS * RUN, :] * row[:, lanes]
        ready[:, :, lanes] = block.reshape(PEERS, RUN, HEAD_WIDTH).astype(jnp.bfloat16)
    pltpu.make_async_copy(ready.at[me], out.at[0, :, mine], out_recv).start()
    for step in range(1, PEERS):
        peer = (me + step) % PEERS
        copy = pltpu.make_async_remote_copy(
            src_ref=ready.at[peer],
            dst_ref=out.at[0, :, mine],
            send_sem=out_send.at[step],
            recv_sem=out_recv,
            device_id=(s, seat(peer)),
            device_id_type=MESH,
        )
        copy.start()
        sends.append((None, copy))

    for condition, copy in sends:
        if condition is None:
            copy.wait_send()
        else:
            pl.when(condition)(copy.wait_send)
    arrival(out, out_recv)


def body(queries, key_value_pages, block_table, page_mask, noise_level, level_gate):
    anywhere = pl.BlockSpec(memory_space=pl.ANY)
    dma = pltpu.SemaphoreType.DMA
    return pl.pallas_call(
        kernel,
        out_shape=jax.ShapeDtypeStruct(queries.shape, jnp.bfloat16),
        in_specs=[
            anywhere,
            anywhere,
            anywhere,
            anywhere,
            pl.BlockSpec(memory_space=pltpu.SMEM),
            anywhere,
        ],
        out_specs=anywhere,
        scratch_shapes=[
            pltpu.VMEM((SPANS, PARTS, 2, PEERS, RUN, HEAD_WIDTH), jnp.bfloat16),
            pltpu.VMEM((PEERS, RUN, WIDE), jnp.bfloat16),
            pltpu.VMEM((ROWS, HEAD_WIDTH), jnp.bfloat16),
            pltpu.VMEM((PEERS, RUN, WIDE), jnp.bfloat16),
            pltpu.VMEM((level_gate.shape[0], WIDE), jnp.float32),
            pltpu.VMEM(key_value_pages.shape[1:], jnp.bfloat16),
            pltpu.VMEM((KEY_VALUE_HEADS, 2, RUN, HEAD_WIDTH), jnp.bfloat16),
            pltpu.VMEM(block_table.shape, jnp.int32),
            pltpu.VMEM(page_mask.shape, jnp.int32),
            pltpu.VMEM((SPANS // 2, PARTS, 8, 128), jnp.float32),
            pltpu.VMEM((ROWS, 1), jnp.float32),
            pltpu.VMEM((ROWS, 1), jnp.float32),
            pltpu.VMEM((ROWS, HEAD_WIDTH), jnp.float32),
            dma((4,)),
            dma((PEERS,)),
            dma,
            dma((PEERS,)),
            dma,
            dma((4,)),
            dma((2,)),
            dma((2,)),
            dma((32,)),
            dma((SPANS, PARTS)),
            dma((32,)),
            dma((SPANS, PARTS)),
            dma((PEERS,)),
            dma,
        ],
        compiler_params=pltpu.CompilerParams(collective_id=0, has_side_effects=True),
    )(queries, key_value_pages, block_table, page_mask, noise_level, level_gate)


def solution(mesh):
    in_specs = (P("section", "seq", None), P("section", "seq", None, None), P(), P(), P(), P())
    out_specs = P("section", "seq", None)
    return jax.shard_map(body, mesh=mesh, in_specs=in_specs, out_specs=out_specs, check_vma=False)
```

time: 50.2 us -> 51 us (1.016)
  the two profiles are of different devices: /device:TPU:3 before, /device:TPU:10 now
where the time goes in v2:
time: 51 us; the launch traced here: 50.8 us
  Pallas kernels  49.3 us (97%)
  local copies, waits for them, and re-layouts  1.47 us (3%)
    pallas_call x1, Pallas kernels, body(): pl.pallas_call(kernel, out_shape=jax.ShapeDtypeStruct(queries.shape, jnp....  49.3 us
    unnamed x1, local copies, waits for them, and re-layouts  1.47 us

profile of v2, /device:TPU:10, one launch (start us, length us, event | category | flops | bytes accessed | tf_op | source)
XLA Modules:
  0.0 50.8 jit_solution(654644538240240363)
XLA Ops:
  0.0 49.3 %shard_map.64 = bf16[1,8,4096]{2,1,0:T(8,128)(2,1)} custom-call(bf16[1,8,4096]{2,1,0:T(8,128)(2,1)} %queries.1, bf16[1,2,4,2048]{3,2,1,0:T(4,128)(2,1)} %pool.1, s32[16,64]{1,0:T(8,128)} %table_any.1, s32[16,1024]{1,0:T(8,128)} %mask_any.1, s32[16]{0:T(128)} %noise.1, f32[16,4096]{1,0:T(8,128)} %gates.1), custom_call_target="tpu_custom_call" | custom-call | tf_op jit(solution)/shard_map/pallas_call | solution.py:384
  49.3 1.5 %copy.8 = bf16[1,8,4096]{2,1,0:T(8,128)(2,1)} copy(bf16[1,8,4096]{2,1,0:T(8,128)(2,1)} %shard_map.64) | data formatting | bytes 131072

commit v3 on v2

--- a/solution.py
+++ b/solution.py
@@ -31,7 +31,7 @@
     pool,
     table_any,
     mask_any,
-    noise,
+    noise_any,
     gates,
     out,
     kv,
@@ -43,6 +43,7 @@
     source,
     table,
     mask,
+    noise,
     bias,
     top,
     total,
@@ -50,11 +51,9 @@
     local_sem,
     spread_send,
     spread_recv,
+    deep_send,
     query_send,
     query_recv,
-    deep_send,
-    deep_recv,
-    half_recv,
     relay_send,
     relay_recv,
     share_send,
@@ -69,23 +68,42 @@
     column, z = t // 16, t % 16
     part = z // 4
     me = column * 4 + z % 4
-
-    def seat(peer):
-        return (peer // 4) * 16 + part * 4 + peer % 4
+    ahead, behind = column * 16 + (z + 4) % 16, column * 16 + (z + 12) % 16
+
+    def seat(peer, block):
+        return (peer // 4) * 16 + block * 4 + peer % 4
 
     def section(xx, yy):
         return (xx * 4 + yy) * 2 + core
 
     up, down = (y + 1) % 4, (y + 3) % 4
     partner = chip * 2 + 1 - core
-    ahead, behind = column * 16 + (z + 4) % 16, column * 16 + (z + 12) % 16
 
     barrier = pltpu.get_barrier_semaphore()
-    near = [(s, seat((me + step) % PEERS)) for step in range(1, PEERS)]
-    near += [(s, ahead), (s, behind)]
-    near += [(other, t) for other in (section(x, up), section(x, down), section(1 - x, y), partner)]
-    for other in near:
-        pl.semaphore_signal(barrier, inc=1, device_id=other, device_id_type=MESH)
+    corner = section(1 - x, (y + 1 + 2 * x) % 4)
+    for other in (section(x, up), section(x, down), section(1 - x, y), corner, partner):
+        pl.semaphore_signal(barrier, inc=1, device_id=(other, t), device_id_type=MESH)
+    for step in range(1, PEERS):
+        pl.semaphore_signal(
+            barrier, inc=1, device_id=(s, seat((me + step) % PEERS, part)), device_id_type=MESH
+        )
+    for block in range(1, PARTS):
+
+        @pl.when((part < block) & (part < 2))
+        def _():
+            for peer in range(PEERS):
+                pl.semaphore_signal(
+                    barrier, inc=1, device_id=(s, seat(peer, block)), device_id_type=MESH
+                )
+
+    @pl.when(part >= 2)
+    def _():
+        pl.semaphore_signal(
+            barrier,
+            inc=1,
+            device_id=(s, column * 16 + (z + 4 * (5 - 2 * part) + 32) % 16),
+            device_id_type=MESH,
+        )
 
     mine = pl.ds(pl.multiple_of(me * WIDE, WIDE), WIDE)
     loads = [
@@ -93,6 +111,7 @@
         pltpu.make_async_copy(table_any, table, local_sem.at[1]),
         pltpu.make_async_copy(mask_any, mask, local_sem.at[2]),
         pltpu.make_async_copy(gates.at[:, mine], gate, local_sem.at[3]),
+        pltpu.make_async_copy(noise_any, noise, local_sem.at[4]),
     ]
     for load in loads:
         load.start()
@@ -114,22 +133,31 @@
     total[...] = jnp.zeros(total.shape, jnp.float32)
     accum[...] = jnp.zeros(accum.shape, jnp.float32)
 
-    pl.semaphore_wait(barrier, len(near))
+    low = part < 2
+    lower = jnp.minimum(part, 2)
+    pl.semaphore_wait(barrier, 12 + PEERS * lower + jnp.where(low, 0, 1))
 
     sends = []
-    pltpu.make_async_copy(source.at[me], kv.at[s, part, :, me], spread_recv).start()
-    for step in range(1, PEERS):
+
+    def spread(turn, step, block, condition):
         peer = (me + step) % PEERS
         copy = pltpu.make_async_remote_copy(
             src_ref=source.at[peer],
             dst_ref=kv.at[s, part, :, me],
-            send_sem=spread_send.at[step],
-            recv_sem=spread_recv,
-            device_id=(s, seat(peer)),
-            device_id_type=MESH,
-        )
-        copy.start()
-        sends.append((None, copy))
+            send_sem=spread_send.at[turn * PEERS + step],
+            recv_sem=spread_recv.at[part],
+            device_id=(s, seat(peer, block)),
+            device_id_type=MESH,
+        )
+        pl.when(condition)(copy.start)
+        sends.append((condition, copy))
+
+    for block in range(2):
+        for step in range(PEERS):
+            spread(block + 1, step, block, block < lower)
+    pltpu.make_async_copy(source.at[me], kv.at[s, part, :, me], spread_recv.at[part]).start()
+    for step in range(1, PEERS):
+        spread(0, step, part, s >= 0)
     for step in range(PEERS):
         peer = (me + step) % PEERS
         piece = queries.at[0, :, pl.ds(pl.multiple_of(peer * WIDE, WIDE), WIDE)]
@@ -141,7 +169,7 @@
             dst_ref=arrived.at[me],
             send_sem=query_send.at[step],
             recv_sem=query_recv,
-            device_id=(s, seat(peer)),
+            device_id=(s, seat(peer, part)),
             device_id_type=MESH,
         )
         copy.start()
@@ -161,18 +189,6 @@
         lanes = slice((c % 2) * 64, (c % 2) * 64 + 64)
         for piece in range(PARTS):
             bias[c // 2, piece, :, lanes] = hide[:, piece * 64 : (piece + 1) * 64]
-
-    def deep(src, number, arrival, other):
-        copy = pltpu.make_async_remote_copy(
-            src_ref=src,
-            dst_ref=src,
-            send_sem=deep_send.at[number],
-            recv_sem=arrival,
-            device_id=(s, other),
-            device_id_type=MESH,
-        )
-        copy.start()
-        sends.append((None, copy))
 
     count = [0, 0]
 
@@ -237,7 +253,35 @@
 
     always = s >= 0
     far = x == 1
-    first, after1, before1, opposite = (part + 0, (part + 1) % 4, (part + 3) % 4, (part + 2) % 4)
+
+    others = [part, (part + 1) % 4, (part + 2) % 4, (part + 3) % 4]
+    for turn in range(1, PARTS):
+        others[turn] = jnp.where(part == 3, (turn + 1) % 3, others[turn])
+
+    def deep(number, piece, other, condition):
+        copy = pltpu.make_async_remote_copy(
+            src_ref=kv.at[s, piece],
+            dst_ref=kv.at[s, piece],
+            send_sem=deep_send.at[number],
+            recv_sem=spread_recv.at[piece],
+            device_id=(s, other),
+            device_id_type=MESH,
+        )
+        pl.when(condition)(copy.start)
+        sends.append((condition, copy))
+
+    def collect(turn):
+        piece = others[turn]
+        arrival(kv.at[s, piece], spread_recv.at[piece])
+        outward(piece)
+        if turn == 0:
+            deep(0, part, column * 16 + (z + 4 * (5 - 2 * part) + 32) % 16, part >= 2)
+        if turn == 1:
+            deep(1, part, ahead, part < 2)
+        if turn == 3:
+            deep(2, part, behind, part == 0)
+            deep(3, others[1], behind, part == 0)
+            deep(4, piece, ahead, part == 1)
 
     def outward(piece):
         relay(s, piece, section(x, up), (x == 0) | (y < 3))
@@ -254,24 +298,20 @@
         landed(slot, piece, gets0)
         relay(slot, piece, section(1, y), x == 0)
         relay(slot, piece, section(x, up), (y == 1) | (y == 2))
+        relay(slot, piece, section(1, up), x == 0)
         share(slot, piece, uses0)
         slot = chip3 * 2 + core
         landed(slot, piece, far)
         relay(slot, piece, section(1, down), far)
         share(slot, piece, far)
 
-    def middle(piece):
-        slot = chip4 * 2 + core
-        landed(slot, piece, far)
-        relay(slot, piece, section(1, up), far)
-        share(slot, piece, far)
-
     def late(piece, which, condition):
         slot = which * 2 + core
         landed(slot, piece, condition)
         share(slot, piece, condition)
 
     def tail(piece):
+        late(piece, chip4, far)
         late(piece, chip1, uses1)
         late(piece, chip2, uses2)
         late(piece, chip5, far)
@@ -296,58 +336,45 @@
 
         attend(chip, pieces, always)
 
-    arrival(kv.at[s, first], spread_recv)
-    deep(kv.at[s, first], 0, deep_recv.at[0], ahead)
-    deep(kv.at[s, first], 1, deep_recv.at[1], behind)
-    outward(first)
-
+    collect(0)
     arrival(arrived, query_recv)
     for head in range(GROUP):
         lanes = slice(head * HEAD_WIDTH, (head + 1) * HEAD_WIDTH)
         tall = arrived[:, :, lanes].astype(jnp.float32).reshape(PEERS * RUN, HEAD_WIDTH)
         rows[head * PEERS * RUN : (head + 1) * PEERS * RUN, :] = tall.astype(jnp.bfloat16)
 
-    early(first)
-    arrival(kv.at[s, before1], deep_recv.at[0])
-    deep(kv.at[s, before1, 0], 2, half_recv.at[0], ahead)
-    outward(before1)
-    arrival(kv.at[s, after1], deep_recv.at[1])
-    deep(kv.at[s, after1, 1], 3, half_recv.at[1], behind)
-    outward(after1)
-    middle(first)
-    early(before1)
-    early(after1)
-    arrival(kv.at[s, opposite, 0], half_recv.at[0])
-    arrival(kv.at[s, opposite, 1], half_recv.at[1])
-    outward(opposite)
-    middle(before1)
-    middle(after1)
-    tail(first)
-    early(opposite)
-    most = (first, before1, after1)
-    own(most)
-    take(chip0, most, uses0)
-    middle(opposite)
-    tail(before1)
-    tail(after1)
-    take(chip3, most, far)
-    take(chip4, most, far)
-    take(chip1, most, uses1)
-    take(chip2, most, uses2)
-    take(chip5, most, far)
-    take(chip6, most, far)
-    last = (opposite,)
-    tail(opposite)
-    own(last)
-    take(chip0, last, uses0)
-    take(chip3, last, far)
-    take(chip4, last, far)
-    take(chip1, last, uses1)
-    take(chip2, last, uses2)
-    take(chip5, last, far)
-    take(chip6, last, far)
+    part0, part1, part2, part3 = others
+    half, rest = (part0, part1), (part2, part3)
+    early(part0)
+    collect(1)
+    tail(part0)
+    early(part1)
+    collect(2)
+    collect(3)
+    own(half)
+    take(chip0, half, uses0)
+    take(chip3, half, far)
+    early(part2)
+    early(part3)
+    tail(part1)
+    take(chip4, half, far)
+    take(chip1, half, uses1)
+    take(chip2, half, uses2)
+    take(chip5, half, far)
+    take(chip6, half, far)
+    own(rest)
+    tail(part2)
+    tail(part3)
+    take(chip0, rest, uses0)
+    take(chip3, rest, far)
+    take(chip4, rest, far)
+    take(chip1, rest, uses1)
+    take(chip2, rest, uses2)
+    take(chip5, rest, far)
+    take(chip6, rest, far)
 
     loads[3].wait()
+    loads[4].wait()
     level = noise[s]
     row = gate[pl.ds(level, 1), :]
     mixed = accum[...] / total[...]
@@ -364,7 +391,7 @@
             dst_ref=out.at[0, :, mine],
             send_sem=out_send.at[step],
             recv_sem=out_recv,
-            device_id=(s, seat(peer)),
+            device_id=(s, seat(peer, part)),
             device_id_type=MESH,
         )
         copy.start()
@@ -378,20 +405,14 @@
     arrival(out, out_recv)
 
 
-def body(queries, key_value_pages, block_table, page_mask, noise_level, level_gate):
+def body(*arrays):
+    queries, key_value_pages, block_table, page_mask, noise_level, level_gate = arrays
     anywhere = pl.BlockSpec(memory_space=pl.ANY)
     dma = pltpu.SemaphoreType.DMA
     return pl.pallas_call(
         kernel,
         out_shape=jax.ShapeDtypeStruct(queries.shape, jnp.bfloat16),
-        in_specs=[
-            anywhere,
-            anywhere,
-            anywhere,
-            anywhere,
-            pl.BlockSpec(memory_space=pltpu.SMEM),
-            anywhere,
-        ],
+        in_specs=[anywhere] * len(arrays),
         out_specs=anywhere,
         scratch_shapes=[
             pltpu.VMEM((SPANS, PARTS, 2, PEERS, RUN, HEAD_WIDTH), jnp.bfloat16),
@@ -403,18 +424,17 @@
             pltpu.VMEM((KEY_VALUE_HEADS, 2, RUN, HEAD_WIDTH), jnp.bfloat16),
             pltpu.VMEM(block_table.shape, jnp.int32),
             pltpu.VMEM(page_mask.shape, jnp.int32),
+            pltpu.SMEM(noise_level.shape, jnp.int32),
             pltpu.VMEM((SPANS // 2, PARTS, 8, 128), jnp.float32),
             pltpu.VMEM((ROWS, 1), jnp.float32),
             pltpu.VMEM((ROWS, 1), jnp.float32),
             pltpu.VMEM((ROWS, HEAD_WIDTH), jnp.float32),
-            dma((4,)),
+            dma((5,)),
+            dma((3 * PEERS,)),
+            dma((PARTS,)),
+            dma((5,)),
             dma((PEERS,)),
             dma,
-            dma((PEERS,)),
-            dma,
-            dma((4,)),
-            dma((2,)),
-            dma((2,)),
             dma((32,)),
             dma((SPANS, PARTS)),
             dma((32,)),
@@ -422,8 +442,10 @@
             dma((PEERS,)),
             dma,
         ],
-        compiler_params=pltpu.CompilerParams(collective_id=0, has_side_effects=True),
-    )(queries, key_value_pages, block_table, page_mask, noise_level, level_gate)
+        compiler_params=pltpu.CompilerParams(
+            collective_id=0, has_side_effects=True, vmem_limit_bytes=16 * 1024 * 1024
+        ),
+    )(*(pltpu.with_memory_space_constraint(array, pltpu.HBM) for array in arrays))
 
 
 def solution(mesh):

time: 51 us -> 44.2 us (0.87)
  the two profiles are of different devices: /device:TPU:10 before, /device:TPU:282 now
where the time goes in v3:
time: 44.2 us; the launch traced here: 44 us
  Pallas kernels  43.4 us (98%)
  local copies, waits for them, and re-layouts  0.63 us (1%)
    pallas_call x1, Pallas kernels, body(): pl.pallas_call(kernel, out_shape=jax.ShapeDtypeStruct(queries.shape, jnp....  43.4 us

profile of v3, /device:TPU:282, one launch (start us, length us, event | category | flops | bytes accessed | tf_op | source)
XLA Modules:
  0.0 44.0 jit_solution(4744083537630923606)
XLA Ops:
  0.0 43.4 %shard_map.64 = bf16[1,8,4096]{2,1,0:T(8,128)(2,1)S(1)} custom-call(bf16[1,8,4096]{2,1,0:T(8,128)(2,1)} %queries.1, bf16[1,2,4,2048]{3,2,1,0:T(4,128)(2,1)} %pool.1, s32[16,64]{1,0:T(8,128)} %table_any.1, s32[16,1024]{1,0:T(8,128)} %mask_any.1, s32[16]{0:T(128)} %noise_any.1, f32[16,4096]{1,0:T(8,128)} %gates.1), custom_call_target="tpu_custom_call" | custom-call | tf_op jit(solution)/shard_map/pallas_call | solution.py:412
  43.4 0.6 %copy.8 = bf16[1,8,4096]{2,1,0:T(8,128)(2,1)} copy(bf16[1,8,4096]{2,1,0:T(8,128)(2,1)S(1)} %shard_map.64) | data formatting | bytes 131072

commit v4 on v3

--- a/solution.py
+++ b/solution.py
@@ -87,23 +87,19 @@
         pl.semaphore_signal(
             barrier, inc=1, device_id=(s, seat((me + step) % PEERS, part)), device_id_type=MESH
         )
-    for block in range(1, PARTS):
-
-        @pl.when((part < block) & (part < 2))
-        def _():
+    @pl.when(part == 0)
+    def _():
+        for block in range(1, PARTS):
             for peer in range(PEERS):
                 pl.semaphore_signal(
                     barrier, inc=1, device_id=(s, seat(peer, block)), device_id_type=MESH
                 )
 
-    @pl.when(part >= 2)
+    beside = jnp.where(part == 3, behind, ahead)
+
+    @pl.when(part > 0)
     def _():
-        pl.semaphore_signal(
-            barrier,
-            inc=1,
-            device_id=(s, column * 16 + (z + 4 * (5 - 2 * part) + 32) % 16),
-            device_id_type=MESH,
-        )
+        pl.semaphore_signal(barrier, inc=1, device_id=(s, beside), device_id_type=MESH)
 
     mine = pl.ds(pl.multiple_of(me * WIDE, WIDE), WIDE)
     loads = [
@@ -133,9 +129,9 @@
     total[...] = jnp.zeros(total.shape, jnp.float32)
     accum[...] = jnp.zeros(accum.shape, jnp.float32)
 
-    low = part < 2
-    lower = jnp.minimum(part, 2)
-    pl.semaphore_wait(barrier, 12 + PEERS * lower + jnp.where(low, 0, 1))
+    expected = 12 + jnp.where(part == 0, 0, PEERS)
+    expected += jnp.where(part == 2, 2, 0) + jnp.where(part == 3, 1, 0)
+    pl.semaphore_wait(barrier, expected)
 
     sends = []
 
@@ -152,9 +148,8 @@
         pl.when(condition)(copy.start)
         sends.append((condition, copy))
 
-    for block in range(2):
-        for step in range(PEERS):
-            spread(block + 1, step, block, block < lower)
+    for step in range(PEERS):
+        spread(1, step, 0, part > 0)
     pltpu.make_async_copy(source.at[me], kv.at[s, part, :, me], spread_recv.at[part]).start()
     for step in range(1, PEERS):
         spread(0, step, part, s >= 0)
@@ -226,37 +221,48 @@
         def _():
             arrival(kv.at[slot, piece], relay_recv.at[slot, piece])
 
-    def attend(which, pieces, condition):
+    def attend(chunks, pieces, condition):
         @pl.when(condition)
         def _():
-            units = [(which * 2 + n, piece) for piece in pieces for n in range(2)]
-            keys, values = (
-                jnp.concatenate(
-                    [kv[a, b, kind].reshape(PEERS * RUN, HEAD_WIDTH) for a, b in units], axis=0
+            scores, values = [], []
+            for which in chunks:
+                units = [(which * 2 + n, piece) for piece in pieces for n in range(2)]
+                keys, value = (
+                    jnp.concatenate(
+                        [kv[a, b, kind].reshape(PEERS * RUN, HEAD_WIDTH) for a, b in units], axis=0
+                    )
+                    for kind in range(2)
                 )
-                for kind in range(2)
-            )
-            hide = jnp.concatenate([bias[which, piece, 0:1, :] for piece in pieces], axis=1)
-            scores = lax.dot_general(
-                rows[...], keys, (((1,), (1,)), ((), ())), preferred_element_type=jnp.float32
-            )
-            scores = scores + hide
+                hide = jnp.concatenate([bias[which, piece, 0:1, :] for piece in pieces], axis=1)
+                score = lax.dot_general(
+                    rows[...], keys, (((1,), (1,)), ((), ())), preferred_element_type=jnp.float32
+                )
+                scores.append(score + hide)
+                values.append(value)
             before = top[...]
-            after = jnp.maximum(before, jnp.max(scores, axis=1, keepdims=True))
+            peak = functools.reduce(jnp.maximum, scores)
+            after = jnp.maximum(before, jnp.max(peak, axis=1, keepdims=True))
             shrink = jnp.exp2((before - after) * EXPONENT)
-            weights = jnp.exp2((scores - after) * EXPONENT)
+            weights = [jnp.exp2((score - after) * EXPONENT) for score in scores]
             top[...] = after
-            total[...] = total[...] * shrink + jnp.sum(weights, axis=1, keepdims=True)
-            accum[...] = accum[...] * shrink + jnp.dot(
-                weights.astype(jnp.bfloat16), values, preferred_element_type=jnp.float32
-            )
+            mass = jnp.sum(functools.reduce(jnp.add, weights), axis=1, keepdims=True)
+            total[...] = total[...] * shrink + mass
+            update = accum[...] * shrink
+            for weight, value in zip(weights, values):
+                update += jnp.dot(
+                    weight.astype(jnp.bfloat16), value, preferred_element_type=jnp.float32
+                )
+            accum[...] = update
 
     always = s >= 0
     far = x == 1
 
-    others = [part, (part + 1) % 4, (part + 2) % 4, (part + 3) % 4]
-    for turn in range(1, PARTS):
-        others[turn] = jnp.where(part == 3, (turn + 1) % 3, others[turn])
+    others = [
+        part,
+        jnp.where(part == 3, 2, part + 1),
+        jnp.where(part == 0, 2, 0),
+        jnp.where(part < 2, 3, 1),
+    ]
 
     def deep(number, piece, other, condition):
         copy = pltpu.make_async_remote_copy(
@@ -275,13 +281,16 @@
         arrival(kv.at[s, piece], spread_recv.at[piece])
         outward(piece)
         if turn == 0:
-            deep(0, part, column * 16 + (z + 4 * (5 - 2 * part) + 32) % 16, part >= 2)
+            deep(0, part, beside, part >= 2)
+            deep(1, part, behind, part == 2)
         if turn == 1:
-            deep(1, part, ahead, part < 2)
+            deep(2, part, ahead, part < 2)
+            deep(3, piece, behind, part == 2)
+        if turn == 2:
+            deep(4, piece, ahead, part == 1)
         if turn == 3:
-            deep(2, part, behind, part == 0)
-            deep(3, others[1], behind, part == 0)
-            deep(4, piece, ahead, part == 1)
+            deep(5, part, behind, part == 0)
+            deep(6, others[1], behind, part == 0)
 
     def outward(piece):
         relay(s, piece, section(x, up), (x == 0) | (y < 3))
@@ -317,7 +326,7 @@
         late(piece, chip5, far)
         late(piece, chip6, far)
 
-    def take(which, pieces, condition):
+    def met(which, pieces, condition):
         slot = which * 2 + 1 - core
         for piece in pieces:
 
@@ -325,16 +334,8 @@
             def _():
                 arrival(kv.at[slot, piece], share_recv.at[slot, piece])
 
-        attend(which, pieces, condition)
-
     def own(pieces):
-        for piece in pieces:
-
-            @pl.when(core == 1)
-            def _():
-                arrival(kv.at[chip * 2, piece], share_recv.at[chip * 2, piece])
-
-        attend(chip, pieces, always)
+        met(chip, pieces, core == 1)
 
     collect(0)
     arrival(arrived, query_recv)
@@ -350,28 +351,39 @@
     tail(part0)
     early(part1)
     collect(2)
+    tail(part1)
     collect(3)
     own(half)
-    take(chip0, half, uses0)
-    take(chip3, half, far)
+    for which in (chip3, chip4, chip5, chip6):
+        met(which, half, far)
+    attend([chip], half, x == 0)
+    attend([chip, chip3, chip4, chip5, chip6], half, far)
     early(part2)
     early(part3)
-    tail(part1)
-    take(chip4, half, far)
-    take(chip1, half, uses1)
-    take(chip2, half, uses2)
-    take(chip5, half, far)
-    take(chip6, half, far)
+    met(chip0, half, uses0)
+    met(chip1, half, uses1)
+    met(chip2, half, uses2)
+    attend([chip0], half, y == 1)
+    attend([chip0, chip2], half, y == 2)
+    attend([chip0, chip1, chip2], half, y == 3)
     own(rest)
+    met(chip0, rest, uses0)
+    met(chip3, rest, far)
+    attend([chip], rest, (x == 0) & (y == 0))
+    attend([chip, chip0], rest, (x == 0) & (y > 0))
+    attend([chip, chip3], rest, far & (y == 0))
+    attend([chip, chip0, chip3], rest, far & (y > 0))
     tail(part2)
     tail(part3)
-    take(chip0, rest, uses0)
-    take(chip3, rest, far)
-    take(chip4, rest, far)
-    take(chip1, rest, uses1)
-    take(chip2, rest, uses2)
-    take(chip5, rest, far)
-    take(chip6, rest, far)
+    met(chip1, rest, uses1)
+    met(chip2, rest, uses2)
+    for which in (chip4, chip5, chip6):
+        met(which, rest, far)
+    attend([chip2], rest, (x == 0) & (y == 2))
+    attend([chip1, chip2], rest, (x == 0) & (y == 3))
+    attend([chip4, chip5, chip6], rest, far & (y < 2))
+    attend([chip4, chip5, chip6, chip2], rest, far & (y == 2))
+    attend([chip4, chip5, chip6, chip1, chip2], rest, far & (y == 3))
 
     loads[3].wait()
     loads[4].wait()
@@ -430,9 +442,9 @@
             pltpu.VMEM((ROWS, 1), jnp.float32),
             pltpu.VMEM((ROWS, HEAD_WIDTH), jnp.float32),
             dma((5,)),
-            dma((3 * PEERS,)),
+            dma((2 * PEERS,)),
             dma((PARTS,)),
-            dma((5,)),
+            dma((7,)),
             dma((PEERS,)),
             dma,
             dma((32,)),

time: 44.2 us -> 43.4 us (0.982)
  the two profiles are of different devices: /device:TPU:282 before, /device:TPU:135 now
where the time goes in v4:
time: 43.4 us; the launch traced here: 43.3 us
  Pallas kernels  42.6 us (98%)
  local copies, waits for them, and re-layouts  0.63 us (1%)
    pallas_call x1, Pallas kernels, body(): pl.pallas_call(kernel, out_shape=jax.ShapeDtypeStruct(queries.shape, jnp....  42.6 us

profile of v4, /device:TPU:135, one launch (start us, length us, event | category | flops | bytes accessed | tf_op | source)
XLA Modules:
  0.0 43.3 jit_solution(8770540734151998989)
XLA Ops:
  0.0 42.6 %shard_map.64 = bf16[1,8,4096]{2,1,0:T(8,128)(2,1)S(1)} custom-call(bf16[1,8,4096]{2,1,0:T(8,128)(2,1)} %queries.1, bf16[1,2,4,2048]{3,2,1,0:T(4,128)(2,1)} %pool.1, s32[16,64]{1,0:T(8,128)} %table_any.1, s32[16,1024]{1,0:T(8,128)} %mask_any.1, s32[16]{0:T(128)} %noise_any.1, f32[16,4096]{1,0:T(8,128)} %gates.1), custom_call_target="tpu_custom_call" | custom-call | tf_op jit(solution)/shard_map/pallas_call | solution.py:424
  42.6 0.6 %copy.8 = bf16[1,8,4096]{2,1,0:T(8,128)(2,1)} copy(bf16[1,8,4096]{2,1,0:T(8,128)(2,1)S(1)} %shard_map.64) | data formatting | bytes 131072

commit v5 on v4

--- a/solution.py
+++ b/solution.py
@@ -49,6 +49,7 @@
     total,
     accum,
     local_sem,
+    ready_sem,
     spread_send,
     spread_recv,
     deep_send,
@@ -70,6 +71,11 @@
     me = column * 4 + z % 4
     ahead, behind = column * 16 + (z + 4) % 16, column * 16 + (z + 12) % 16
 
+    def fellow(step):
+        turn = (0, 2, 1, 3, 2, 1, 3, 0)[step]
+        side = (me // 4 + (0 if step in (0, 4, 5, 6) else 1)) % 2
+        return side * 4 + (me + turn) % 4
+
     def seat(peer, block):
         return (peer // 4) * 16 + block * 4 + peer % 4
 
@@ -81,11 +87,13 @@
 
     barrier = pltpu.get_barrier_semaphore()
     corner = section(1 - x, (y + 1 + 2 * x) % 4)
-    for other in (section(x, up), section(x, down), section(1 - x, y), corner, partner):
+    flip = 1 - 2 * core
+    cross = [other + flip for other in (section(x, up), section(x, down), corner)]
+    for other in (section(x, up), section(x, down), section(1 - x, y), corner, partner, *cross):
         pl.semaphore_signal(barrier, inc=1, device_id=(other, t), device_id_type=MESH)
     for step in range(1, PEERS):
         pl.semaphore_signal(
-            barrier, inc=1, device_id=(s, seat((me + step) % PEERS, part)), device_id_type=MESH
+            barrier, inc=1, device_id=(s, seat(fellow(step), part)), device_id_type=MESH
         )
     @pl.when(part == 0)
     def _():
@@ -95,7 +103,7 @@
                     barrier, inc=1, device_id=(s, seat(peer, block)), device_id_type=MESH
                 )
 
-    beside = jnp.where(part == 3, behind, ahead)
+    beside = jnp.where(part % 3 == 0, behind, ahead)
 
     @pl.when(part > 0)
     def _():
@@ -129,17 +137,26 @@
     total[...] = jnp.zeros(total.shape, jnp.float32)
     accum[...] = jnp.zeros(accum.shape, jnp.float32)
 
-    expected = 12 + jnp.where(part == 0, 0, PEERS)
-    expected += jnp.where(part == 2, 2, 0) + jnp.where(part == 3, 1, 0)
-    pl.semaphore_wait(barrier, expected)
+    inner = (part == 1) | (part == 2)
+    extra = jnp.where(part == 2, 2, 0) + jnp.where(part == 3, 1, 0)
+    pl.semaphore_wait(barrier, 15 + jnp.where(part > 0, PEERS, 0) + extra)
+
+    @pl.when(inner)
+    def _():
+        pl.semaphore_signal(ready_sem.at[0], inc=1, device_id=(s, behind), device_id_type=MESH)
+
+    @pl.when(part == 3)
+    def _():
+        pl.semaphore_signal(ready_sem.at[1], inc=1, device_id=(s, ahead), device_id_type=MESH)
 
     sends = []
 
-    def spread(turn, step, block, condition):
-        peer = (me + step) % PEERS
+    def spread(turn, step, block, condition, kind=None):
+        peer = fellow(step)
+        whole = kind is None
         copy = pltpu.make_async_remote_copy(
-            src_ref=source.at[peer],
-            dst_ref=kv.at[s, part, :, me],
+            src_ref=source.at[peer] if whole else source.at[peer, kind],
+            dst_ref=kv.at[s, part, :, me] if whole else kv.at[s, part, kind, me],
             send_sem=spread_send.at[turn * PEERS + step],
             recv_sem=spread_recv.at[part],
             device_id=(s, seat(peer, block)),
@@ -149,27 +166,11 @@
         sends.append((condition, copy))
 
     for step in range(PEERS):
-        spread(1, step, 0, part > 0)
+        spread(1, step, 0, inner)
+        spread(1, step, 0, part == 3, 0)
     pltpu.make_async_copy(source.at[me], kv.at[s, part, :, me], spread_recv.at[part]).start()
     for step in range(1, PEERS):
         spread(0, step, part, s >= 0)
-    for step in range(PEERS):
-        peer = (me + step) % PEERS
-        piece = queries.at[0, :, pl.ds(pl.multiple_of(peer * WIDE, WIDE), WIDE)]
-        if step == 0:
-            pltpu.make_async_copy(piece, arrived.at[me], query_recv).start()
-            continue
-        copy = pltpu.make_async_remote_copy(
-            src_ref=piece,
-            dst_ref=arrived.at[me],
-            send_sem=query_send.at[step],
-            recv_sem=query_recv,
-            device_id=(s, seat(peer, part)),
-            device_id_type=MESH,
-        )
-        copy.start()
-        sends.append((None, copy))
-
     loads[1].wait()
     loads[2].wait()
     place = lax.broadcasted_iota(jnp.int32, (SPAN, PAGES), 0)
@@ -187,12 +188,13 @@
 
     count = [0, 0]
 
-    def relay(slot, piece, other, condition):
+    def relay(slot, piece, other, condition, arrivals=None):
+        arrivals = relay_recv if arrivals is None else arrivals
         copy = pltpu.make_async_remote_copy(
             src_ref=kv.at[slot, piece],
             dst_ref=kv.at[slot, piece],
             send_sem=relay_send.at[count[0]],
-            recv_sem=relay_recv.at[slot, piece],
+            recv_sem=arrivals.at[slot, piece],
             device_id=(other, t),
             device_id_type=MESH,
         )
@@ -259,15 +261,16 @@
 
     others = [
         part,
-        jnp.where(part == 3, 2, part + 1),
-        jnp.where(part == 0, 2, 0),
-        jnp.where(part < 2, 3, 1),
+        1 - part % 2,
+        jnp.where(part == 2, 3, 2),
+        jnp.where(part < 2, 3, part - 2),
     ]
 
-    def deep(number, piece, other, condition):
+    def deep(number, piece, other, condition, kind=None):
+        ref = kv.at[s, piece] if kind is None else kv.at[s, piece, kind]
         copy = pltpu.make_async_remote_copy(
-            src_ref=kv.at[s, piece],
-            dst_ref=kv.at[s, piece],
+            src_ref=ref,
+            dst_ref=ref,
             send_sem=deep_send.at[number],
             recv_sem=spread_recv.at[piece],
             device_id=(s, other),
@@ -281,50 +284,55 @@
         arrival(kv.at[s, piece], spread_recv.at[piece])
         outward(piece)
         if turn == 0:
-            deep(0, part, beside, part >= 2)
-            deep(1, part, behind, part == 2)
+            deep(0, part, ahead, part == 2)
+            deep(0, part, ahead, part == 3, 1)
+            deep(1, part, behind, part >= 2)
         if turn == 1:
-            deep(2, part, ahead, part < 2)
-            deep(3, piece, behind, part == 2)
+            deep(4, piece, beside, part < 2)
         if turn == 2:
-            deep(4, piece, ahead, part == 1)
+            deep(5, piece, behind, part == 2, 0)
         if turn == 3:
-            deep(5, part, behind, part == 0)
-            deep(6, others[1], behind, part == 0)
+            deep(6, piece, ahead, part == 0, 1)
+
+    def twice(slot, piece, other, condition, double):
+        relay(slot, piece, other, condition)
+        if double:
+            relay(slot, piece, other + flip, condition, share_recv)
 
     def outward(piece):
         relay(s, piece, section(x, up), (x == 0) | (y < 3))
         relay(s, piece, section(1, y), x == 0)
         relay(s, piece, section(x, down), y == 0)
+        relay(s, piece, section(1, up), x == 0)
         share(s, piece, core == 0)
 
     chip0, chip1, chip2 = x * 4 + down, x * 4, x * 4 + (y + 2) % 4
     chip3, chip4, chip5, chip6 = y, down, up, (y + 2) % 4
     gets0, uses0, uses1, uses2 = (x == 0) | (y >= 1), y >= 1, y == 3, y >= 2
 
-    def early(piece):
+    def early(piece, double=False):
         slot = chip0 * 2 + core
         landed(slot, piece, gets0)
-        relay(slot, piece, section(1, y), x == 0)
-        relay(slot, piece, section(x, up), (y == 1) | (y == 2))
-        relay(slot, piece, section(1, up), x == 0)
+        twice(slot, piece, section(x, up), (y == 1) | (y == 2), double)
+        twice(slot, piece, section(1, up), x == 0, double)
         share(slot, piece, uses0)
         slot = chip3 * 2 + core
         landed(slot, piece, far)
-        relay(slot, piece, section(1, down), far)
+        twice(slot, piece, section(1, down), far, double)
         share(slot, piece, far)
 
-    def late(piece, which, condition):
+    def late(piece, which, condition, passed=True):
         slot = which * 2 + core
         landed(slot, piece, condition)
-        share(slot, piece, condition)
-
-    def tail(piece):
+        if passed:
+            share(slot, piece, condition)
+
+    def tail(piece, passed=True):
         late(piece, chip4, far)
         late(piece, chip1, uses1)
-        late(piece, chip2, uses2)
-        late(piece, chip5, far)
-        late(piece, chip6, far)
+        late(piece, chip2, uses2, passed)
+        late(piece, chip5, far, passed)
+        late(piece, chip6, far, passed)
 
     def met(which, pieces, condition):
         slot = which * 2 + 1 - core
@@ -338,34 +346,68 @@
         met(chip, pieces, core == 1)
 
     collect(0)
+    for step in range(PEERS):
+        peer = fellow(step)
+        piece = queries.at[0, :, pl.ds(pl.multiple_of(peer * WIDE, WIDE), WIDE)]
+        if step == 0:
+            pltpu.make_async_copy(piece, arrived.at[me], query_recv).start()
+            continue
+        copy = pltpu.make_async_remote_copy(
+            src_ref=piece,
+            dst_ref=arrived.at[me],
+            send_sem=query_send.at[step],
+            recv_sem=query_recv,
+            device_id=(s, seat(peer, part)),
+            device_id_type=MESH,
+        )
+        copy.start()
+        sends.append((None, copy))
+
+    part0, part1, part2, part3 = others
+    half, rest = (part0, part1), (part2, part3)
+    @pl.when(part < 2)
+    def _():
+        pl.semaphore_wait(ready_sem.at[0], 1)
+
+    deep(2, part, ahead, part < 2)
+    early(part0)
+
+    @pl.when(part == 0)
+    def _():
+        pl.semaphore_wait(ready_sem.at[1], 1)
+
+    deep(3, part, behind, part == 0)
+    collect(1)
+    tail(part0)
+    early(part1)
+    collect(2)
     arrival(arrived, query_recv)
     for head in range(GROUP):
         lanes = slice(head * HEAD_WIDTH, (head + 1) * HEAD_WIDTH)
         tall = arrived[:, :, lanes].astype(jnp.float32).reshape(PEERS * RUN, HEAD_WIDTH)
         rows[head * PEERS * RUN : (head + 1) * PEERS * RUN, :] = tall.astype(jnp.bfloat16)
 
-    part0, part1, part2, part3 = others
-    half, rest = (part0, part1), (part2, part3)
-    early(part0)
-    collect(1)
-    tail(part0)
-    early(part1)
-    collect(2)
     tail(part1)
+    early(part2)
+
+    def begin():
+        own(half)
+        for which in (chip3, chip4, chip5, chip6):
+            met(which, half, far)
+        attend([chip], half, x == 0)
+        attend([chip, chip3, chip4, chip5, chip6], half, far)
+        met(chip0, half, uses0)
+        met(chip1, half, uses1)
+        met(chip2, half, uses2)
+        attend([chip0], half, y == 1)
+        attend([chip0, chip2], half, y == 2)
+        attend([chip0, chip1, chip2], half, y == 3)
+
+    pl.when(part == 1)(begin)
     collect(3)
-    own(half)
-    for which in (chip3, chip4, chip5, chip6):
-        met(which, half, far)
-    attend([chip], half, x == 0)
-    attend([chip, chip3, chip4, chip5, chip6], half, far)
-    early(part2)
-    early(part3)
-    met(chip0, half, uses0)
-    met(chip1, half, uses1)
-    met(chip2, half, uses2)
-    attend([chip0], half, y == 1)
-    attend([chip0, chip2], half, y == 2)
-    attend([chip0, chip1, chip2], half, y == 3)
+    pl.when(part != 1)(begin)
+    early(part3, True)
+    tail(part2)
     own(rest)
     met(chip0, rest, uses0)
     met(chip3, rest, far)
@@ -373,8 +415,7 @@
     attend([chip, chip0], rest, (x == 0) & (y > 0))
     attend([chip, chip3], rest, far & (y == 0))
     attend([chip, chip0, chip3], rest, far & (y > 0))
-    tail(part2)
-    tail(part3)
+    tail(part3, False)
     met(chip1, rest, uses1)
     met(chip2, rest, uses2)
     for which in (chip4, chip5, chip6):
@@ -397,7 +438,7 @@
         ready[:, :, lanes] = block.reshape(PEERS, RUN, HEAD_WIDTH).astype(jnp.bfloat16)
     pltpu.make_async_copy(ready.at[me], out.at[0, :, mine], out_recv).start()
     for step in range(1, PEERS):
-        peer = (me + step) % PEERS
+        peer = fellow(step)
         copy = pltpu.make_async_remote_copy(
             src_ref=ready.at[peer],
             dst_ref=out.at[0, :, mine],
@@ -442,6 +483,7 @@
             pltpu.VMEM((ROWS, 1), jnp.float32),
             pltpu.VMEM((ROWS, HEAD_WIDTH), jnp.float32),
             dma((5,)),
+            pltpu.SemaphoreType.REGULAR((2,)),
             dma((2 * PEERS,)),
             dma((PARTS,)),
             dma((7,)),

time: 43.4 us -> 42.3 us (0.975)
  the two profiles are of different devices: /device:TPU:135 before, /device:TPU:144 now
where the time goes in v5:
time: 42.3 us; the launch traced here: 42.2 us
  Pallas kernels  41.5 us (98%)
  local copies, waits for them, and re-layouts  0.63 us (1%)
    pallas_call x1, Pallas kernels, body(): pl.pallas_call(kernel, out_shape=jax.ShapeDtypeStruct(queries.shape, jnp....  41.5 us

profile of v5, /device:TPU:144, one launch (start us, length us, event | category | flops | bytes accessed | tf_op | source)
XLA Modules:
  0.0 42.2 jit_solution(6218277131942409524)
XLA Ops:
  0.0 41.5 %shard_map.64 = bf16[1,8,4096]{2,1,0:T(8,128)(2,1)S(1)} custom-call(bf16[1,8,4096]{2,1,0:T(8,128)(2,1)} %queries.1, bf16[1,2,4,2048]{3,2,1,0:T(4,128)(2,1)} %pool.1, s32[16,64]{1,0:T(8,128)} %table_any.1, s32[16,1024]{1,0:T(8,128)} %mask_any.1, s32[16]{0:T(128)} %noise_any.1, f32[16,4096]{1,0:T(8,128)} %gates.1), custom_call_target="tpu_custom_call" | custom-call | tf_op jit(solution)/shard_map/pallas_call | solution.py:465
  41.5 0.6 %copy.8 = bf16[1,8,4096]{2,1,0:T(8,128)(2,1)} copy(bf16[1,8,4096]{2,1,0:T(8,128)(2,1)S(1)} %shard_map.64) | data formatting | bytes 131072

commit v6 on v5

--- a/solution.py
+++ b/solution.py
@@ -408,6 +408,21 @@
     pl.when(part != 1)(begin)
     early(part3, True)
     tail(part2)
+    late(part3, chip4, far)
+    late(part3, chip1, uses1)
+
+    def finish(piece):
+        met(chip1, piece, uses1)
+        met(chip2, piece, uses2)
+        for which in (chip4, chip5, chip6):
+            met(which, piece, far)
+        attend([chip2], piece, (x == 0) & (y == 2))
+        attend([chip1, chip2], piece, (x == 0) & (y == 3))
+        attend([chip4, chip5, chip6], piece, far & (y < 2))
+        attend([chip4, chip5, chip6, chip2], piece, far & (y == 2))
+        attend([chip4, chip5, chip6, chip1, chip2], piece, far & (y == 3))
+
+    finish((part2,))
     own(rest)
     met(chip0, rest, uses0)
     met(chip3, rest, far)
@@ -415,16 +430,10 @@
     attend([chip, chip0], rest, (x == 0) & (y > 0))
     attend([chip, chip3], rest, far & (y == 0))
     attend([chip, chip0, chip3], rest, far & (y > 0))
-    tail(part3, False)
-    met(chip1, rest, uses1)
-    met(chip2, rest, uses2)
-    for which in (chip4, chip5, chip6):
-        met(which, rest, far)
-    attend([chip2], rest, (x == 0) & (y == 2))
-    attend([chip1, chip2], rest, (x == 0) & (y == 3))
-    attend([chip4, chip5, chip6], rest, far & (y < 2))
-    attend([chip4, chip5, chip6, chip2], rest, far & (y == 2))
-    attend([chip4, chip5, chip6, chip1, chip2], rest, far & (y == 3))
+    late(part3, chip2, uses2, False)
+    late(part3, chip5, far, False)
+    late(part3, chip6, far, False)
+    finish((part3,))
 
     loads[3].wait()
     loads[4].wait()

time: 42.3 us -> 42.2 us (level)
  no operation moved by 1% of the time
where the time goes in v6:
time: 42.2 us; the launch traced here: 42.1 us
  Pallas kernels  41.4 us (98%)
  local copies, waits for them, and re-layouts  0.63 us (1%)
    pallas_call x1, Pallas kernels, body(): pl.pallas_call(kernel, out_shape=jax.ShapeDtypeStruct(queries.shape, jnp....  41.4 us

profile of v6, /device:TPU:144, one launch (start us, length us, event | category | flops | bytes accessed | tf_op | source)
XLA Modules:
  0.0 42.1 jit_solution(4208187145022300268)
XLA Ops:
  0.0 41.4 %shard_map.64 = bf16[1,8,4096]{2,1,0:T(8,128)(2,1)S(1)} custom-call(bf16[1,8,4096]{2,1,0:T(8,128)(2,1)} %queries.1, bf16[1,2,4,2048]{3,2,1,0:T(4,128)(2,1)} %pool.1, s32[16,64]{1,0:T(8,128)} %table_any.1, s32[16,1024]{1,0:T(8,128)} %mask_any.1, s32[16]{0:T(128)} %noise_any.1, f32[16,4096]{1,0:T(8,128)} %gates.1), custom_call_target="tpu_custom_call" | custom-call | tf_op jit(solution)/shard_map/pallas_call | solution.py:474
  41.5 0.6 %copy.8 = bf16[1,8,4096]{2,1,0:T(8,128)(2,1)} copy(bf16[1,8,4096]{2,1,0:T(8,128)(2,1)S(1)} %shard_map.64) | data formatting | bytes 131072

commit v7 on v5

--- a/solution.py
+++ b/solution.py
@@ -88,7 +88,8 @@
     barrier = pltpu.get_barrier_semaphore()
     corner = section(1 - x, (y + 1 + 2 * x) % 4)
     flip = 1 - 2 * core
-    cross = [other + flip for other in (section(x, up), section(x, down), corner)]
+    beyond = (section(x, up), section(x, down), section(1 - x, y), corner)
+    cross = [other + flip for other in beyond]
     for other in (section(x, up), section(x, down), section(1 - x, y), corner, partner, *cross):
         pl.semaphore_signal(barrier, inc=1, device_id=(other, t), device_id_type=MESH)
     for step in range(1, PEERS):
@@ -139,7 +140,7 @@
 
     inner = (part == 1) | (part == 2)
     extra = jnp.where(part == 2, 2, 0) + jnp.where(part == 3, 1, 0)
-    pl.semaphore_wait(barrier, 15 + jnp.where(part > 0, PEERS, 0) + extra)
+    pl.semaphore_wait(barrier, 16 + jnp.where(part > 0, PEERS, 0) + extra)
 
     @pl.when(inner)
     def _():
@@ -282,7 +283,7 @@
     def collect(turn):
         piece = others[turn]
         arrival(kv.at[s, piece], spread_recv.at[piece])
-        outward(piece)
+        outward(piece, turn == 3)
         if turn == 0:
             deep(0, part, ahead, part == 2)
             deep(0, part, ahead, part == 3, 1)
@@ -299,11 +300,13 @@
         if double:
             relay(slot, piece, other + flip, condition, share_recv)
 
-    def outward(piece):
+    def outward(piece, double=False):
         relay(s, piece, section(x, up), (x == 0) | (y < 3))
-        relay(s, piece, section(1, y), x == 0)
-        relay(s, piece, section(x, down), y == 0)
-        relay(s, piece, section(1, up), x == 0)
+        twice(s, piece, section(1, y), x == 0, double)
+        twice(s, piece, section(x, down), y == 0, double)
+        twice(s, piece, section(1, up), x == 0, double)
+        if double:
+            relay(s, piece, section(x, up) + flip, y < 3, share_recv)
         share(s, piece, core == 0)
 
     chip0, chip1, chip2 = x * 4 + down, x * 4, x * 4 + (y + 2) % 4
@@ -315,11 +318,13 @@
         landed(slot, piece, gets0)
         twice(slot, piece, section(x, up), (y == 1) | (y == 2), double)
         twice(slot, piece, section(1, up), x == 0, double)
-        share(slot, piece, uses0)
+        if not double:
+            share(slot, piece, uses0)
         slot = chip3 * 2 + core
         landed(slot, piece, far)
         twice(slot, piece, section(1, down), far, double)
-        share(slot, piece, far)
+        if not double:
+            share(slot, piece, far)
 
     def late(piece, which, condition, passed=True):
         slot = which * 2 + core
@@ -328,8 +333,8 @@
             share(slot, piece, condition)
 
     def tail(piece, passed=True):
-        late(piece, chip4, far)
-        late(piece, chip1, uses1)
+        late(piece, chip4, far, passed)
+        late(piece, chip1, uses1, passed)
         late(piece, chip2, uses2, passed)
         late(piece, chip5, far, passed)
         late(piece, chip6, far, passed)
@@ -489,7 +494,7 @@
             dma((7,)),
             dma((PEERS,)),
             dma,
-            dma((32,)),
+            dma((64,)),
             dma((SPANS, PARTS)),
             dma((32,)),
             dma((SPANS, PARTS)),

time: 42.3 us -> 42.6 us (level)
  no operation moved by 1% of the time
where the time goes in v7:
time: 42.6 us; the launch traced here: 42.5 us
  Pallas kernels  41.8 us (98%)
  local copies, waits for them, and re-layouts  0.63 us (1%)
    pallas_call x1, Pallas kernels, body(): pl.pallas_call(kernel, out_shape=jax.ShapeDtypeStruct(queries.shape, jnp....  41.8 us

profile of v7, /device:TPU:144, one launch (start us, length us, event | category | flops | bytes accessed | tf_op | source)
XLA Modules:
  0.0 42.5 jit_solution(4374650077854346207)
XLA Ops:
  0.0 41.8 %shard_map.64 = bf16[1,8,4096]{2,1,0:T(8,128)(2,1)S(1)} custom-call(bf16[1,8,4096]{2,1,0:T(8,128)(2,1)} %queries.1, bf16[1,2,4,2048]{3,2,1,0:T(4,128)(2,1)} %pool.1, s32[16,64]{1,0:T(8,128)} %table_any.1, s32[16,1024]{1,0:T(8,128)} %mask_any.1, s32[16]{0:T(128)} %noise_any.1, f32[16,4096]{1,0:T(8,128)} %gates.1), custom_call_target="tpu_custom_call" | custom-call | tf_op jit(solution)/shard_map/pallas_call | solution.py:470
  41.8 0.6 %copy.8 = bf16[1,8,4096]{2,1,0:T(8,128)(2,1)} copy(bf16[1,8,4096]{2,1,0:T(8,128)(2,1)S(1)} %shard_map.64) | data formatting | bytes 131072

commit v8 on v5

--- a/solution.py
+++ b/solution.py
@@ -186,6 +186,13 @@
         for piece in range(PARTS):
             bias[c // 2, piece, :, lanes] = hide[:, piece * 64 : (piece + 1) * 64]
 
+    def drain(copies):
+        for condition, copy in copies:
+            if condition is None:
+                copy.wait_send()
+            else:
+                pl.when(condition)(copy.wait_send)
+
     count = [0, 0]
 
     def relay(slot, piece, other, condition, arrivals=None):
@@ -380,6 +387,7 @@
     collect(1)
     tail(part0)
     early(part1)
+    started = len(sends)
     collect(2)
     arrival(arrived, query_recv)
     for head in range(GROUP):
@@ -408,6 +416,7 @@
     pl.when(part != 1)(begin)
     early(part3, True)
     tail(part2)
+    drain(sends[:started])
     own(rest)
     met(chip0, rest, uses0)
     met(chip3, rest, far)
@@ -450,11 +459,7 @@
         copy.start()
         sends.append((None, copy))
 
-    for condition, copy in sends:
-        if condition is None:
-            copy.wait_send()
-        else:
-            pl.when(condition)(copy.wait_send)
+    drain(sends[started:])
     arrival(out, out_recv)
 
 

time: 42.3 us -> 42.3 us (level)
  no operation moved by 1% of the time
where the time goes in v8:
time: 42.3 us; the launch traced here: 42.2 us
  Pallas kernels  41.5 us (98%)
  local copies, waits for them, and re-layouts  0.63 us (1%)
    pallas_call x1, Pallas kernels, body(): pl.pallas_call(kernel, out_shape=jax.ShapeDtypeStruct(queries.shape, jnp....  41.5 us

profile of v8, /device:TPU:144, one launch (start us, length us, event | category | flops | bytes accessed | tf_op | source)
XLA Modules:
  0.0 42.2 jit_solution(3340343385838445933)
XLA Ops:
  0.0 41.5 %shard_map.64 = bf16[1,8,4096]{2,1,0:T(8,128)(2,1)S(1)} custom-call(bf16[1,8,4096]{2,1,0:T(8,128)(2,1)} %queries.1, bf16[1,2,4,2048]{3,2,1,0:T(4,128)(2,1)} %pool.1, s32[16,64]{1,0:T(8,128)} %table_any.1, s32[16,1024]{1,0:T(8,128)} %mask_any.1, s32[16]{0:T(128)} %noise_any.1, f32[16,4096]{1,0:T(8,128)} %gates.1), custom_call_target="tpu_custom_call" | custom-call | tf_op jit(solution)/shard_map/pallas_call | solution.py:470
  41.5 0.6 %copy.8 = bf16[1,8,4096]{2,1,0:T(8,128)(2,1)} copy(bf16[1,8,4096]{2,1,0:T(8,128)(2,1)S(1)} %shard_map.64) | data formatting | bytes 131072
